TPU v7x, 256 devices: a whole 4x4x8 slice. The times are simulated.
256 devices in a mesh: dp: 2 (over core), ctx: 32 (over z, y), head: 4 (over x).
Axes of the slice: x: 4, y: 4, z: 8, core: 2. Of those that a mesh axis runs over, the one named last changes fastest.
Arguments:
- queries: bfloat16 [2, 32768, 2048], P('dp', 'ctx', 'head'), may hold values from -6 to 6
- keys_raw: bfloat16 [2, 32768, 2048], P('dp', 'ctx', 'head'), may hold values from -0.625 to 0.625
- values: bfloat16 [2, 32768, 2048], P('dp', 'ctx', 'head'), may hold values from -6 to 6
- gates: float32 [2, 16, 32768], P('dp', 'head', 'ctx'), as said below
- lengths: int32 [2, 16], P('dp'), may hold values from 1 to 8192, 32768 in all within a row
- key_gain: float32 [16, 128], P('head'), may hold values from 0.1 to 1.9
- cotangent: bfloat16 [2, 32768, 2048], P('dp', 'ctx', 'head'), may hold values from -6 to 6
Outputs:
- attended: bfloat16 [2, 32768, 2048], P('dp', 'ctx', 'head')
- grad_queries: bfloat16 [2, 32768, 2048], P('dp', 'ctx', 'head')
- grad_keys: bfloat16 [2, 32768, 2048], P('dp', 'ctx', 'head')
- grad_values: bfloat16 [2, 32768, 2048], P('dp', 'ctx', 'head')
- grad_gates: float32 [2, 16, 32768], P('dp', 'head', 'ctx')
- grad_gain: float32 [16, 128], P('head', 'dp')
Inputs may be any that keep to these rules, and one draw needn't show every extreme that they name: Each row of lengths gives its documents in packing order and sums to 32768. `gates`: every entry is negative.
All inputs are finite; a program needn't handle non-finite values.
Results may differ from a plain program's by a relative error of at most 0.009.
Values sent between devices are 32-bit elements; how exact they have to be, the bound alone decides.
A program may use at most 128 MiB of HBM per device.

v0:
```python
import jax
import jax.numpy as jnp
from jax import lax
from jax.sharding import PartitionSpec as P

BLOCK = 512
PRECISE = lax.Precision.HIGHEST


def passed_along(value, axis, steps):
    count = lax.axis_size(axis)
    first, last = (max(0, -steps), min(count, count - steps))
    return lax.ppermute(value, axis, [(source, source + steps) for source in range(first, last)])


def start_flags(doc_lengths, first_pos, num_rows):
    starts = jnp.cumsum(doc_lengths, dtype=jnp.int32) - doc_lengths
    positions = first_pos + jnp.arange(num_rows, dtype=jnp.int32)
    matches = jnp.any(positions[:, None] == starts[None, :], axis=1)
    return matches.astype(jnp.float32)


def make_step(key_gain, head_width):
    q_scale = head_width ** (-0.5)

    def block_step(carried, inputs):
        q_block, k_block, v_block, gate_block, flag_block = inputs
        k_bf = (k_block.astype(jnp.float32) * key_gain[None]).astype(jnp.bfloat16)
        q_float = q_block.astype(jnp.float32) * q_scale
        k_float = lax.optimization_barrier(k_bf).astype(jnp.float32)
        v_float = v_block.astype(jnp.float32)
        segment = jnp.cumsum(flag_block)
        positions = jnp.arange(flag_block.shape[0])
        same_doc = (segment[:, None] == segment[None, :]) & (
            positions[:, None] >= positions[None, :]
        )
        cum_decay = jnp.cumsum(gate_block, axis=1)
        exponent = cum_decay[:, :, None] - cum_decay[:, None, :]
        decays = jnp.where(same_doc[None], jnp.exp(jnp.where(same_doc[None], exponent, 0.0)), 0.0)
        scores = jnp.einsum("thd,shd->hts", q_block, k_bf, preferred_element_type=jnp.float32)
        weights = (scores * q_scale * decays).astype(jnp.bfloat16)
        within = jnp.einsum("hts,she->the", weights, v_block, preferred_element_type=jnp.float32)
        opened = (segment == 0).astype(cum_decay.dtype)
        carry_in = jnp.exp(cum_decay) * opened[None, :]
        across = (
            jnp.einsum("thd,hde->the", q_float, carried, precision=PRECISE) * carry_in.T[:, :, None]
        )
        tail_mask = (segment == segment[-1]).astype(cum_decay.dtype)
        to_end = jnp.exp(cum_decay[:, -1:] - cum_decay) * tail_mask[None, :]
        written = jnp.einsum(
            "shd,she->hde", k_float * to_end.T[:, :, None], v_float, precision=PRECISE
        )
        end_state = carried * carry_in[:, -1][:, None, None] + written
        return (end_state, within + across)

    return block_step


def run_blocks(q_rows, k_rows, v_rows, gate_rows, flags, key_gain, start_state):
    num_rows = q_rows.shape[0]
    head_count = key_gain.shape[0]
    head_width = key_gain.shape[1]
    num_blocks = num_rows // BLOCK

    def to_blocks(tensor):
        return tensor.reshape(num_blocks, BLOCK, head_count, head_width)

    gate_blocks = gate_rows.reshape(head_count, num_blocks, BLOCK).transpose(1, 0, 2)
    flag_blocks = flags.reshape(num_blocks, BLOCK)
    end_state, outputs = lax.scan(
        jax.checkpoint(make_step(key_gain, head_width)),
        start_state,
        (to_blocks(q_rows), to_blocks(k_rows), to_blocks(v_rows), gate_blocks, flag_blocks),
    )
    return (outputs.reshape(num_rows, head_count * head_width), end_state)


def shards(queries, keys_raw, values, gates, lengths, key_gain, cotangent):
    tok_rows = queries.shape[1]
    head_count = key_gain.shape[0]
    head_width = key_gain.shape[1]
    flags = start_flags(lengths[0], lax.axis_index("ctx") * tok_rows, tok_rows)
    q_rows, k_rows, v_rows, gate_rows = (queries[0], keys_raw[0], values[0], gates[0])
    segment = jnp.cumsum(flags)
    opened = (segment == 0).astype(jnp.float32)
    tail_mask = (segment == segment[-1]).astype(jnp.float32)
    cum_decay = jnp.cumsum(gate_rows, axis=1)
    shard_decay = jnp.exp(cum_decay[:, -1]) * opened[-1]
    to_end = jnp.exp(cum_decay[:, -1:] - cum_decay) * tail_mask[None, :]
    k_bf = (
        k_rows.reshape(tok_rows, head_count, head_width).astype(jnp.float32) * key_gain[None]
    ).astype(jnp.bfloat16)
    k_float = lax.optimization_barrier(k_bf).astype(jnp.float32)
    v_float = v_rows.reshape(tok_rows, head_count, head_width).astype(jnp.float32)
    local_end = jnp.einsum(
        "shd,she->hde", k_float * to_end.T[:, :, None], v_float, precision=PRECISE
    )
    ctx_size = lax.axis_size("ctx")

    def relay_forward(step_index, incoming):
        return passed_along(shard_decay[:, None, None] * incoming + local_end, "ctx", 1)

    state_in = lax.fori_loop(0, ctx_size - 1, relay_forward, jnp.zeros_like(local_end))

    def forward(q_part, k_part, v_part, gate_part, gain_part):
        return run_blocks(q_part, k_part, v_part, gate_part, flags, gain_part, state_in)

    (primal, end_state), pullback = jax.vjp(forward, q_rows, k_rows, v_rows, gate_rows, key_gain)
    factor = jnp.exp(cum_decay) * opened[None, :]
    weighted = (
        q_rows.reshape(tok_rows, head_count, head_width).astype(jnp.float32)
        * head_width ** (-0.5)
        * factor.T[:, :, None]
    )
    cot_float = cotangent[0].astype(jnp.float32)
    local_grad = jnp.einsum(
        "thd,the->hde",
        weighted,
        cot_float.reshape(tok_rows, head_count, head_width),
        precision=PRECISE,
    )

    def relay_back(step_index, incoming):
        return passed_along(shard_decay[:, None, None] * incoming + local_grad, "ctx", -1)

    later_grad = lax.fori_loop(0, ctx_size - 1, relay_back, jnp.zeros_like(local_grad))
    grad_q, grad_k, grad_v, grad_a, gain_term = pullback((cot_float, later_grad))
    gain_total = lax.psum(gain_term, "ctx")
    grad_gain = lax.psum_scatter(gain_total, "dp", scatter_dimension=1, tiled=True)
    return (
        primal.astype(jnp.bfloat16)[None],
        grad_q[None],
        grad_k[None],
        grad_v[None],
        grad_a[None],
        grad_gain,
    )


def solution(mesh):
    placed = (
        P("dp", "ctx", "head"),
        P("dp", "ctx", "head"),
        P("dp", "ctx", "head"),
        P("dp", "head", "ctx"),
        P("dp", None),
        P("head", None),
        P("dp", "ctx", "head"),
    )
    return jax.shard_map(
        shards,
        mesh=mesh,
        in_specs=placed,
        out_specs=(
            P("dp", "ctx", "head"),
            P("dp", "ctx", "head"),
            P("dp", "ctx", "head"),
            P("dp", "ctx", "head"),
            P("dp", "head", "ctx"),
            P("head", "dp"),
        ),
        check_vma=False,
    )
```

profile of v0, /device:TPU:2, one launch (start us, length us, event | category | flops | bytes accessed | tf_op | source)
XLA Modules:
  0.0 1009.6 jit_solution(5768768737271364331)
XLA Ops:
  37.1 336.8 %while.62 = (s32[]{:T(128)}, f32[4,128,128]{2,1,0:T(8,128)S(1)}, f32[4]{0:T(128)S(1)}, f32[4,128,128]{2,1,0:T(8,128)S(1)}, s32[]{:T(128)}) while((s32[]{:T(128)}, f32[4,128,128]{2,1,0:T(8,128)S(1)}, f32[4]{0:T(128)S(1)}, f32[4,128,128]{2,1,0:T(8,128)S(1)}, s32[]{:T(128)}) %tuple.140), condition=%wide.region_7.8_spmd, body=%wide.region_6.7_spmd.sunk | while | flops 131074 | bytes 1835125 | solution.py:103
  90.1 6.5 collective-permute-start
  100.6 6.9 collective-permute-start
  112.6 7.1 collective-permute-start
  119.7 6.2 collective-permute-done
  126.0 7.4 collective-permute-start
  133.4 6.0 collective-permute-done
  139.5 6.5 collective-permute-start
  160.6 6.5 collective-permute-start
  171.1 6.5 collective-permute-start
  181.5 6.5 collective-permute-start
  192.0 6.5 collective-permute-start
  202.7 6.8 collective-permute-start
  214.7 7.1 collective-permute-start
  221.9 6.3 collective-permute-done
  228.3 7.5 collective-permute-start
  241.7 6.2 collective-permute-start
  262.2 6.5 collective-permute-start
  272.7 6.5 collective-permute-start
  283.2 6.5 collective-permute-start
  293.6 6.5 collective-permute-start
  304.5 6.8 collective-permute-start
  316.8 7.1 collective-permute-start
  323.9 6.5 collective-permute-done
  330.5 7.2 collective-permute-start
  343.4 6.2 collective-permute-start
  353.6 5.9 collective-permute-start
  363.5 6.5 collective-permute-start
  373.8 27.3 %while.64 = (s32[]{:T(128)}, f32[4,128,128]{2,1,0:T(8,128)S(1)}, bf16[2,512,4,128]{1,3,2,0:T(8,128)(2,1)}, f32[2,4,128,128]{3,2,1,0:T(8,128)}, f32[2,4,512]{2,1,...) while((s32[]{:T(128)}, f32[4,128,128]{2,1,0:T(8,128)S(1)}, ...), condition=%wide.region_13.14_spmd.clone, body=%wide.region_8.13_spmd.clone.sunk | while | flops 1352081408 | bytes 9343697 | solution.py:70
  404.3 365.5 %while.63 = (s32[]{:T(128)}, f32[4,128,128]{2,1,0:T(8,128)S(1)}, f32[4]{0:T(128)S(1)}, f32[4,128,128]{2,1,0:T(8,128)S(1)}, s32[]{:T(128)}) while((s32[]{:T(128)}, f32[4,128,128]{2,1,0:T(8,128)S(1)}, f32[4]{0:T(128)S(1)}, f32[4,128,128]{2,1,0:T(8,128)S(1)}, s32[]{:T(128)}) %tuple.160), condition=%wide.region_15.16_spmd, body=%wide.region_14.15_spmd.sunk | while | flops 131074 | bytes 1835125 | solution.py:126
  405.7 9.5 collective-permute-done.1
  416.7 9.5 collective-permute-done.1
  427.6 9.7 collective-permute-done.1
  438.7 11.9 %collective-permute-done.1 = f32[4,128,128]{2,1,0:T(8,128)S(1)} collective-permute-done((f32[4,128,128]{2,1,0:T(8,128)S(1)}, f32[4,128,128]{2,1,0:T(8,128)S(1)}, u32[]{:S(2)}, u32[]{:S(2)}) %collective-permute-start.1) | collective-permute-done | bytes 262176 | tf_op jit(solution)/shard_map/while/body/eval_jaxpr/ppermute | solution.py:13
  451.9 12.8 %collective-permute-done.1 = f32[4,128,128]{2,1,0:T(8,128)S(1)} collective-permute-done((f32[4,128,128]{2,1,0:T(8,128)S(1)}, f32[4,128,128]{2,1,0:T(8,128)S(1)}, u32[]{:S(2)}, u32[]{:S(2)}) %collective-permute-start.1) | collective-permute-done | bytes 262176 | tf_op jit(solution)/shard_map/while/body/eval_jaxpr/ppermute | solution.py:13
  466.2 11.3 %collective-permute-done.1 = f32[4,128,128]{2,1,0:T(8,128)S(1)} collective-permute-done((f32[4,128,128]{2,1,0:T(8,128)S(1)}, f32[4,128,128]{2,1,0:T(8,128)S(1)}, u32[]{:S(2)}, u32[]{:S(2)}) %collective-permute-start.1) | collective-permute-done | bytes 262176 | tf_op jit(solution)/shard_map/while/body/eval_jaxpr/ppermute | solution.py:13
  478.8 10.0 collective-permute-done.1
  490.3 10.6 %collective-permute-done.1 = f32[4,128,128]{2,1,0:T(8,128)S(1)} collective-permute-done((f32[4,128,128]{2,1,0:T(8,128)S(1)}, f32[4,128,128]{2,1,0:T(8,128)S(1)}, u32[]{:S(2)}, u32[]{:S(2)}) %collective-permute-start.1) | collective-permute-done | bytes 262176 | tf_op jit(solution)/shard_map/while/body/eval_jaxpr/ppermute | solution.py:13
  502.3 9.8 collective-permute-done.1
  513.5 9.2 collective-permute-done.1
  524.1 8.7 collective-permute-done.1
  534.2 10.4 %collective-permute-done.1 = f32[4,128,128]{2,1,0:T(8,128)S(1)} collective-permute-done((f32[4,128,128]{2,1,0:T(8,128)S(1)}, f32[4,128,128]{2,1,0:T(8,128)S(1)}, u32[]{:S(2)}, u32[]{:S(2)}) %collective-permute-start.1) | collective-permute-done | bytes 262176 | tf_op jit(solution)/shard_map/while/body/eval_jaxpr/ppermute | solution.py:13
  545.9 10.6 %collective-permute-done.1 = f32[4,128,128]{2,1,0:T(8,128)S(1)} collective-permute-done((f32[4,128,128]{2,1,0:T(8,128)S(1)}, f32[4,128,128]{2,1,0:T(8,128)S(1)}, u32[]{:S(2)}, u32[]{:S(2)}) %collective-permute-start.1) | collective-permute-done | bytes 262176 | tf_op jit(solution)/shard_map/while/body/eval_jaxpr/ppermute | solution.py:13
  557.9 9.6 collective-permute-done.1
  568.9 8.1 collective-permute-done.1
  578.5 8.5 collective-permute-done.1
  588.4 9.6 collective-permute-done.1
  599.3 11.3 %collective-permute-done.1 = f32[4,128,128]{2,1,0:T(8,128)S(1)} collective-permute-done((f32[4,128,128]{2,1,0:T(8,128)S(1)}, f32[4,128,128]{2,1,0:T(8,128)S(1)}, u32[]{:S(2)}, u32[]{:S(2)}) %collective-permute-start.1) | collective-permute-done | bytes 262176 | tf_op jit(solution)/shard_map/while/body/eval_jaxpr/ppermute | solution.py:13
  612.0 9.3 collective-permute-done.1
  622.7 10.2 %collective-permute-done.1 = f32[4,128,128]{2,1,0:T(8,128)S(1)} collective-permute-done((f32[4,128,128]{2,1,0:T(8,128)S(1)}, f32[4,128,128]{2,1,0:T(8,128)S(1)}, u32[]{:S(2)}, u32[]{:S(2)}) %collective-permute-start.1) | collective-permute-done | bytes 262176 | tf_op jit(solution)/shard_map/while/body/eval_jaxpr/ppermute | solution.py:13
  634.4 16.1 %collective-permute-done.1 = f32[4,128,128]{2,1,0:T(8,128)S(1)} collective-permute-done((f32[4,128,128]{2,1,0:T(8,128)S(1)}, f32[4,128,128]{2,1,0:T(8,128)S(1)}, u32[]{:S(2)}, u32[]{:S(2)}) %collective-permute-start.1) | collective-permute-done | bytes 262176 | tf_op jit(solution)/shard_map/while/body/eval_jaxpr/ppermute | solution.py:13
  651.9 11.2 %collective-permute-done.1 = f32[4,128,128]{2,1,0:T(8,128)S(1)} collective-permute-done((f32[4,128,128]{2,1,0:T(8,128)S(1)}, f32[4,128,128]{2,1,0:T(8,128)S(1)}, u32[]{:S(2)}, u32[]{:S(2)}) %collective-permute-start.1) | collective-permute-done | bytes 262176 | tf_op jit(solution)/shard_map/while/body/eval_jaxpr/ppermute | solution.py:13
  664.5 12.7 %collective-permute-done.1 = f32[4,128,128]{2,1,0:T(8,128)S(1)} collective-permute-done((f32[4,128,128]{2,1,0:T(8,128)S(1)}, f32[4,128,128]{2,1,0:T(8,128)S(1)}, u32[]{:S(2)}, u32[]{:S(2)}) %collective-permute-start.1) | collective-permute-done | bytes 262176 | tf_op jit(solution)/shard_map/while/body/eval_jaxpr/ppermute | solution.py:13
  678.6 10.0 collective-permute-done.1
  690.0 8.4 collective-permute-done.1
  699.8 10.7 %collective-permute-done.1 = f32[4,128,128]{2,1,0:T(8,128)S(1)} collective-permute-done((f32[4,128,128]{2,1,0:T(8,128)S(1)}, f32[4,128,128]{2,1,0:T(8,128)S(1)}, u32[]{:S(2)}, u32[]{:S(2)}) %collective-permute-start.1) | collective-permute-done | bytes 262176 | tf_op jit(solution)/shard_map/while/body/eval_jaxpr/ppermute | solution.py:13
  711.9 10.4 %collective-permute-done.1 = f32[4,128,128]{2,1,0:T(8,128)S(1)} collective-permute-done((f32[4,128,128]{2,1,0:T(8,128)S(1)}, f32[4,128,128]{2,1,0:T(8,128)S(1)}, u32[]{:S(2)}, u32[]{:S(2)}) %collective-permute-start.1) | collective-permute-done | bytes 262176 | tf_op jit(solution)/shard_map/while/body/eval_jaxpr/ppermute | solution.py:13
  723.8 10.9 %collective-permute-done.1 = f32[4,128,128]{2,1,0:T(8,128)S(1)} collective-permute-done((f32[4,128,128]{2,1,0:T(8,128)S(1)}, f32[4,128,128]{2,1,0:T(8,128)S(1)}, u32[]{:S(2)}, u32[]{:S(2)}) %collective-permute-start.1) | collective-permute-done | bytes 262176 | tf_op jit(solution)/shard_map/while/body/eval_jaxpr/ppermute | solution.py:13
  736.1 9.6 collective-permute-done.1
  747.1 10.2 %collective-permute-done.1 = f32[4,128,128]{2,1,0:T(8,128)S(1)} collective-permute-done((f32[4,128,128]{2,1,0:T(8,128)S(1)}, f32[4,128,128]{2,1,0:T(8,128)S(1)}, u32[]{:S(2)}, u32[]{:S(2)}) %collective-permute-start.1) | collective-permute-done | bytes 262176 | tf_op jit(solution)/shard_map/while/body/eval_jaxpr/ppermute | solution.py:13
  758.7 11.2 %collective-permute-done.1 = f32[4,128,128]{2,1,0:T(8,128)S(1)} collective-permute-done((f32[4,128,128]{2,1,0:T(8,128)S(1)}, f32[4,128,128]{2,1,0:T(8,128)S(1)}, u32[]{:S(2)}, u32[]{:S(2)}) %collective-permute-start.1) | collective-permute-done | bytes 262176 | tf_op jit(solution)/shard_map/while/body/eval_jaxpr/ppermute | solution.py:13
  773.6 85.2 %while.65 = (s32[]{:T(128)}, f32[4,128]{1,0:T(4,128)S(1)}, f32[4,128,128]{2,1,0:T(8,128)S(1)}, bf16[2,512,4,128]{3,2,1,0:T(4,128)(2,1)}, bf16[2,512,4,128]{3,2,1...) while((s32[]{:T(128)}, f32[4,128]{1,0:T(4,128)S(1)}, ...), condition=%wide.region_30.31_spmd.clone, body=%wide.region_16.30_spmd.clone.sunk | while | flops 3394863616 | bytes 116524784 | solution.py:70
  867.9 58.3 %reduce-scatter.4.cloned.1.call-done = f32[64,4]{1,0:T(8,128)} async-done(((f32[128,4]{1,0:T(8,128)}), f32[64,4]{1,0:T(8,128)}) %reduce-scatter.4.cloned.1.call-update) | async-done | bytes 1040
  927.1 75.7 %psum.8 = f32[4,64]{1,0:T(4,128)} all-reduce(f32[4,64]{1,0:T(4,128)S(1)} %copy.251), channel_id=1, replica_groups=mesh['dp'=2,'ctx'=32,'head'=4] {'ctx'}, use_global_device_ids=true, to_apply=%region_31.32 | all-reduce | flops 256 | bytes 2048 | tf_op jit(solution)/shard_map/psum | solution.py:128
  (406 shorter events, 358.7 us)
Async XLA Ops:
  7.2 919.1 %reduce-scatter.4.cloned.1.call-start = ((), (), s32[]{:S(2)}) async-start(), calls=%async_computation.1 | async-start | bytes 98304
  16.4 9.8 copy-start.18
  37.2 9.0 collective-permute-start
  46.3 9.1 collective-permute-start
  55.5 8.3 collective-permute-start
  63.8 8.3 collective-permute-start
  72.2 8.3 collective-permute-start
  80.6 9.5 collective-permute-start
  90.1 10.4 %collective-permute-start = (f32[4,128,128]{2,1,0:T(8,128)S(1)}, f32[4,128,128]{2,1,0:T(8,128)S(1)}, u32[]{:S(2)}, u32[]{:S(2)}) collective-permute-start(f32[4,128,128]{2,1,0:T(8,128)S(1)} %multiply_add_fusion.4), channel_id=1, source_target_pairs={{0,4},{4,8},{8,12},{12,16},{16,20},{20,24},{24,28},{28,32},{32,36}... | collective-permute-start | bytes 786440 | tf_op jit(solution)/shard_map/while/body/eval_jaxpr/ppermute | solution.py:13
  100.6 11.9 %collective-permute-start = (f32[4,128,128]{2,1,0:T(8,128)S(1)}, f32[4,128,128]{2,1,0:T(8,128)S(1)}, u32[]{:S(2)}, u32[]{:S(2)}) collective-permute-start(f32[4,128,128]{2,1,0:T(8,128)S(1)} %multiply_add_fusion.4), channel_id=1, source_target_pairs={{0,4},{4,8},{8,12},{12,16},{16,20},{20,24},{24,28},{28,32},{32,36}... | collective-permute-start | bytes 786440 | tf_op jit(solution)/shard_map/while/body/eval_jaxpr/ppermute | solution.py:13
  112.6 13.4 %collective-permute-start = (f32[4,128,128]{2,1,0:T(8,128)S(1)}, f32[4,128,128]{2,1,0:T(8,128)S(1)}, u32[]{:S(2)}, u32[]{:S(2)}) collective-permute-start(f32[4,128,128]{2,1,0:T(8,128)S(1)} %multiply_add_fusion.4), channel_id=1, source_target_pairs={{0,4},{4,8},{8,12},{12,16},{16,20},{20,24},{24,28},{28,32},{32,36}... | collective-permute-start | bytes 786440 | tf_op jit(solution)/shard_map/while/body/eval_jaxpr/ppermute | solution.py:13
  126.0 13.4 %collective-permute-start = (f32[4,128,128]{2,1,0:T(8,128)S(1)}, f32[4,128,128]{2,1,0:T(8,128)S(1)}, u32[]{:S(2)}, u32[]{:S(2)}) collective-permute-start(f32[4,128,128]{2,1,0:T(8,128)S(1)} %multiply_add_fusion.4), channel_id=1, source_target_pairs={{0,4},{4,8},{8,12},{12,16},{16,20},{20,24},{24,28},{28,32},{32,36}... | collective-permute-start | bytes 786440 | tf_op jit(solution)/shard_map/while/body/eval_jaxpr/ppermute | solution.py:13
  139.5 11.2 %collective-permute-start = (f32[4,128,128]{2,1,0:T(8,128)S(1)}, f32[4,128,128]{2,1,0:T(8,128)S(1)}, u32[]{:S(2)}, u32[]{:S(2)}) collective-permute-start(f32[4,128,128]{2,1,0:T(8,128)S(1)} %multiply_add_fusion.4), channel_id=1, source_target_pairs={{0,4},{4,8},{8,12},{12,16},{16,20},{20,24},{24,28},{28,32},{32,36}... | collective-permute-start | bytes 786440 | tf_op jit(solution)/shard_map/while/body/eval_jaxpr/ppermute | solution.py:13
  150.9 9.6 collective-permute-start
  160.6 10.4 %collective-permute-start = (f32[4,128,128]{2,1,0:T(8,128)S(1)}, f32[4,128,128]{2,1,0:T(8,128)S(1)}, u32[]{:S(2)}, u32[]{:S(2)}) collective-permute-start(f32[4,128,128]{2,1,0:T(8,128)S(1)} %multiply_add_fusion.4), channel_id=1, source_target_pairs={{0,4},{4,8},{8,12},{12,16},{16,20},{20,24},{24,28},{28,32},{32,36}... | collective-permute-start | bytes 786440 | tf_op jit(solution)/shard_map/while/body/eval_jaxpr/ppermute | solution.py:13
  171.1 10.4 %collective-permute-start = (f32[4,128,128]{2,1,0:T(8,128)S(1)}, f32[4,128,128]{2,1,0:T(8,128)S(1)}, u32[]{:S(2)}, u32[]{:S(2)}) collective-permute-start(f32[4,128,128]{2,1,0:T(8,128)S(1)} %multiply_add_fusion.4), channel_id=1, source_target_pairs={{0,4},{4,8},{8,12},{12,16},{16,20},{20,24},{24,28},{28,32},{32,36}... | collective-permute-start | bytes 786440 | tf_op jit(solution)/shard_map/while/body/eval_jaxpr/ppermute | solution.py:13
  181.5 10.4 %collective-permute-start = (f32[4,128,128]{2,1,0:T(8,128)S(1)}, f32[4,128,128]{2,1,0:T(8,128)S(1)}, u32[]{:S(2)}, u32[]{:S(2)}) collective-permute-start(f32[4,128,128]{2,1,0:T(8,128)S(1)} %multiply_add_fusion.4), channel_id=1, source_target_pairs={{0,4},{4,8},{8,12},{12,16},{16,20},{20,24},{24,28},{28,32},{32,36}... | collective-permute-start | bytes 786440 | tf_op jit(solution)/shard_map/while/body/eval_jaxpr/ppermute | solution.py:13
  192.0 10.6 %collective-permute-start = (f32[4,128,128]{2,1,0:T(8,128)S(1)}, f32[4,128,128]{2,1,0:T(8,128)S(1)}, u32[]{:S(2)}, u32[]{:S(2)}) collective-permute-start(f32[4,128,128]{2,1,0:T(8,128)S(1)} %multiply_add_fusion.4), channel_id=1, source_target_pairs={{0,4},{4,8},{8,12},{12,16},{16,20},{20,24},{24,28},{28,32},{32,36}... | collective-permute-start | bytes 786440 | tf_op jit(solution)/shard_map/while/body/eval_jaxpr/ppermute | solution.py:13
  202.7 11.9 %collective-permute-start = (f32[4,128,128]{2,1,0:T(8,128)S(1)}, f32[4,128,128]{2,1,0:T(8,128)S(1)}, u32[]{:S(2)}, u32[]{:S(2)}) collective-permute-start(f32[4,128,128]{2,1,0:T(8,128)S(1)} %multiply_add_fusion.4), channel_id=1, source_target_pairs={{0,4},{4,8},{8,12},{12,16},{16,20},{20,24},{24,28},{28,32},{32,36}... | collective-permute-start | bytes 786440 | tf_op jit(solution)/shard_map/while/body/eval_jaxpr/ppermute | solution.py:13
  214.7 13.5 %collective-permute-start = (f32[4,128,128]{2,1,0:T(8,128)S(1)}, f32[4,128,128]{2,1,0:T(8,128)S(1)}, u32[]{:S(2)}, u32[]{:S(2)}) collective-permute-start(f32[4,128,128]{2,1,0:T(8,128)S(1)} %multiply_add_fusion.4), channel_id=1, source_target_pairs={{0,4},{4,8},{8,12},{12,16},{16,20},{20,24},{24,28},{28,32},{32,36}... | collective-permute-start | bytes 786440 | tf_op jit(solution)/shard_map/while/body/eval_jaxpr/ppermute | solution.py:13
  228.3 13.3 %collective-permute-start = (f32[4,128,128]{2,1,0:T(8,128)S(1)}, f32[4,128,128]{2,1,0:T(8,128)S(1)}, u32[]{:S(2)}, u32[]{:S(2)}) collective-permute-start(f32[4,128,128]{2,1,0:T(8,128)S(1)} %multiply_add_fusion.4), channel_id=1, source_target_pairs={{0,4},{4,8},{8,12},{12,16},{16,20},{20,24},{24,28},{28,32},{32,36}... | collective-permute-start | bytes 786440 | tf_op jit(solution)/shard_map/while/body/eval_jaxpr/ppermute | solution.py:13
  241.7 10.8 %collective-permute-start = (f32[4,128,128]{2,1,0:T(8,128)S(1)}, f32[4,128,128]{2,1,0:T(8,128)S(1)}, u32[]{:S(2)}, u32[]{:S(2)}) collective-permute-start(f32[4,128,128]{2,1,0:T(8,128)S(1)} %multiply_add_fusion.4), channel_id=1, source_target_pairs={{0,4},{4,8},{8,12},{12,16},{16,20},{20,24},{24,28},{28,32},{32,36}... | collective-permute-start | bytes 786440 | tf_op jit(solution)/shard_map/while/body/eval_jaxpr/ppermute | solution.py:13
  252.6 9.6 collective-permute-start
  262.2 10.4 %collective-permute-start = (f32[4,128,128]{2,1,0:T(8,128)S(1)}, f32[4,128,128]{2,1,0:T(8,128)S(1)}, u32[]{:S(2)}, u32[]{:S(2)}) collective-permute-start(f32[4,128,128]{2,1,0:T(8,128)S(1)} %multiply_add_fusion.4), channel_id=1, source_target_pairs={{0,4},{4,8},{8,12},{12,16},{16,20},{20,24},{24,28},{28,32},{32,36}... | collective-permute-start | bytes 786440 | tf_op jit(solution)/shard_map/while/body/eval_jaxpr/ppermute | solution.py:13
  272.7 10.4 %collective-permute-start = (f32[4,128,128]{2,1,0:T(8,128)S(1)}, f32[4,128,128]{2,1,0:T(8,128)S(1)}, u32[]{:S(2)}, u32[]{:S(2)}) collective-permute-start(f32[4,128,128]{2,1,0:T(8,128)S(1)} %multiply_add_fusion.4), channel_id=1, source_target_pairs={{0,4},{4,8},{8,12},{12,16},{16,20},{20,24},{24,28},{28,32},{32,36}... | collective-permute-start | bytes 786440 | tf_op jit(solution)/shard_map/while/body/eval_jaxpr/ppermute | solution.py:13
  283.2 10.4 %collective-permute-start = (f32[4,128,128]{2,1,0:T(8,128)S(1)}, f32[4,128,128]{2,1,0:T(8,128)S(1)}, u32[]{:S(2)}, u32[]{:S(2)}) collective-permute-start(f32[4,128,128]{2,1,0:T(8,128)S(1)} %multiply_add_fusion.4), channel_id=1, source_target_pairs={{0,4},{4,8},{8,12},{12,16},{16,20},{20,24},{24,28},{28,32},{32,36}... | collective-permute-start | bytes 786440 | tf_op jit(solution)/shard_map/while/body/eval_jaxpr/ppermute | solution.py:13
  293.6 10.8 %collective-permute-start = (f32[4,128,128]{2,1,0:T(8,128)S(1)}, f32[4,128,128]{2,1,0:T(8,128)S(1)}, u32[]{:S(2)}, u32[]{:S(2)}) collective-permute-start(f32[4,128,128]{2,1,0:T(8,128)S(1)} %multiply_add_fusion.4), channel_id=1, source_target_pairs={{0,4},{4,8},{8,12},{12,16},{16,20},{20,24},{24,28},{28,32},{32,36}... | collective-permute-start | bytes 786440 | tf_op jit(solution)/shard_map/while/body/eval_jaxpr/ppermute | solution.py:13
  304.5 12.2 %collective-permute-start = (f32[4,128,128]{2,1,0:T(8,128)S(1)}, f32[4,128,128]{2,1,0:T(8,128)S(1)}, u32[]{:S(2)}, u32[]{:S(2)}) collective-permute-start(f32[4,128,128]{2,1,0:T(8,128)S(1)} %multiply_add_fusion.4), channel_id=1, source_target_pairs={{0,4},{4,8},{8,12},{12,16},{16,20},{20,24},{24,28},{28,32},{32,36}... | collective-permute-start | bytes 786440 | tf_op jit(solution)/shard_map/while/body/eval_jaxpr/ppermute | solution.py:13
  316.8 13.6 %collective-permute-start = (f32[4,128,128]{2,1,0:T(8,128)S(1)}, f32[4,128,128]{2,1,0:T(8,128)S(1)}, u32[]{:S(2)}, u32[]{:S(2)}) collective-permute-start(f32[4,128,128]{2,1,0:T(8,128)S(1)} %multiply_add_fusion.4), channel_id=1, source_target_pairs={{0,4},{4,8},{8,12},{12,16},{16,20},{20,24},{24,28},{28,32},{32,36}... | collective-permute-start | bytes 786440 | tf_op jit(solution)/shard_map/while/body/eval_jaxpr/ppermute | solution.py:13
  330.5 12.8 %collective-permute-start = (f32[4,128,128]{2,1,0:T(8,128)S(1)}, f32[4,128,128]{2,1,0:T(8,128)S(1)}, u32[]{:S(2)}, u32[]{:S(2)}) collective-permute-start(f32[4,128,128]{2,1,0:T(8,128)S(1)} %multiply_add_fusion.4), channel_id=1, source_target_pairs={{0,4},{4,8},{8,12},{12,16},{16,20},{20,24},{24,28},{28,32},{32,36}... | collective-permute-start | bytes 786440 | tf_op jit(solution)/shard_map/while/body/eval_jaxpr/ppermute | solution.py:13
  343.4 10.1 %collective-permute-start = (f32[4,128,128]{2,1,0:T(8,128)S(1)}, f32[4,128,128]{2,1,0:T(8,128)S(1)}, u32[]{:S(2)}, u32[]{:S(2)}) collective-permute-start(f32[4,128,128]{2,1,0:T(8,128)S(1)} %multiply_add_fusion.4), channel_id=1, source_target_pairs={{0,4},{4,8},{8,12},{12,16},{16,20},{20,24},{24,28},{28,32},{32,36}... | collective-permute-start | bytes 786440 | tf_op jit(solution)/shard_map/while/body/eval_jaxpr/ppermute | solution.py:13
  353.6 9.7 collective-permute-start
  363.5 10.4 %collective-permute-start = (f32[4,128,128]{2,1,0:T(8,128)S(1)}, f32[4,128,128]{2,1,0:T(8,128)S(1)}, u32[]{:S(2)}, u32[]{:S(2)}) collective-permute-start(f32[4,128,128]{2,1,0:T(8,128)S(1)} %multiply_add_fusion.4), channel_id=1, source_target_pairs={{0,4},{4,8},{8,12},{12,16},{16,20},{20,24},{24,28},{28,32},{32,36}... | collective-permute-start | bytes 786440 | tf_op jit(solution)/shard_map/while/body/eval_jaxpr/ppermute | solution.py:13
  404.4 10.8 %collective-permute-start.1 = (f32[4,128,128]{2,1,0:T(8,128)S(1)}, f32[4,128,128]{2,1,0:T(8,128)S(1)}, u32[]{:S(2)}, u32[]{:S(2)}) collective-permute-start(f32[4,128,128]{2,1,0:T(8,128)S(1)} %multiply_add_fusion.5), channel_id=1, source_target_pairs={{4,0},{8,4},{12,8},{16,12},{20,16},{24,20},{28,24},{32,28},{36,32}... | collective-permute-start | bytes 786440 | tf_op jit(solution)/shard_map/while/body/eval_jaxpr/ppermute | solution.py:13
  415.4 10.8 %collective-permute-start.1 = (f32[4,128,128]{2,1,0:T(8,128)S(1)}, f32[4,128,128]{2,1,0:T(8,128)S(1)}, u32[]{:S(2)}, u32[]{:S(2)}) collective-permute-start(f32[4,128,128]{2,1,0:T(8,128)S(1)} %multiply_add_fusion.5), channel_id=1, source_target_pairs={{4,0},{8,4},{12,8},{16,12},{20,16},{24,20},{28,24},{32,28},{36,32}... | collective-permute-start | bytes 786440 | tf_op jit(solution)/shard_map/while/body/eval_jaxpr/ppermute | solution.py:13
  426.3 11.0 %collective-permute-start.1 = (f32[4,128,128]{2,1,0:T(8,128)S(1)}, f32[4,128,128]{2,1,0:T(8,128)S(1)}, u32[]{:S(2)}, u32[]{:S(2)}) collective-permute-start(f32[4,128,128]{2,1,0:T(8,128)S(1)} %multiply_add_fusion.5), channel_id=1, source_target_pairs={{4,0},{8,4},{12,8},{16,12},{20,16},{24,20},{28,24},{32,28},{36,32}... | collective-permute-start | bytes 786440 | tf_op jit(solution)/shard_map/while/body/eval_jaxpr/ppermute | solution.py:13
  437.3 13.2 %collective-permute-start.1 = (f32[4,128,128]{2,1,0:T(8,128)S(1)}, f32[4,128,128]{2,1,0:T(8,128)S(1)}, u32[]{:S(2)}, u32[]{:S(2)}) collective-permute-start(f32[4,128,128]{2,1,0:T(8,128)S(1)} %multiply_add_fusion.5), channel_id=1, source_target_pairs={{4,0},{8,4},{12,8},{16,12},{20,16},{24,20},{28,24},{32,28},{36,32}... | collective-permute-start | bytes 786440 | tf_op jit(solution)/shard_map/while/body/eval_jaxpr/ppermute | solution.py:13
  450.6 14.1 %collective-permute-start.1 = (f32[4,128,128]{2,1,0:T(8,128)S(1)}, f32[4,128,128]{2,1,0:T(8,128)S(1)}, u32[]{:S(2)}, u32[]{:S(2)}) collective-permute-start(f32[4,128,128]{2,1,0:T(8,128)S(1)} %multiply_add_fusion.5), channel_id=1, source_target_pairs={{4,0},{8,4},{12,8},{16,12},{20,16},{24,20},{28,24},{32,28},{36,32}... | collective-permute-start | bytes 786440 | tf_op jit(solution)/shard_map/while/body/eval_jaxpr/ppermute | solution.py:13
  464.8 12.6 %collective-permute-start.1 = (f32[4,128,128]{2,1,0:T(8,128)S(1)}, f32[4,128,128]{2,1,0:T(8,128)S(1)}, u32[]{:S(2)}, u32[]{:S(2)}) collective-permute-start(f32[4,128,128]{2,1,0:T(8,128)S(1)} %multiply_add_fusion.5), channel_id=1, source_target_pairs={{4,0},{8,4},{12,8},{16,12},{20,16},{24,20},{28,24},{32,28},{36,32}... | collective-permute-start | bytes 786440 | tf_op jit(solution)/shard_map/while/body/eval_jaxpr/ppermute | solution.py:13
  477.5 11.3 %collective-permute-start.1 = (f32[4,128,128]{2,1,0:T(8,128)S(1)}, f32[4,128,128]{2,1,0:T(8,128)S(1)}, u32[]{:S(2)}, u32[]{:S(2)}) collective-permute-start(f32[4,128,128]{2,1,0:T(8,128)S(1)} %multiply_add_fusion.5), channel_id=1, source_target_pairs={{4,0},{8,4},{12,8},{16,12},{20,16},{24,20},{28,24},{32,28},{36,32}... | collective-permute-start | bytes 786440 | tf_op jit(solution)/shard_map/while/body/eval_jaxpr/ppermute | solution.py:13
  489.0 11.9 %collective-permute-start.1 = (f32[4,128,128]{2,1,0:T(8,128)S(1)}, f32[4,128,128]{2,1,0:T(8,128)S(1)}, u32[]{:S(2)}, u32[]{:S(2)}) collective-permute-start(f32[4,128,128]{2,1,0:T(8,128)S(1)} %multiply_add_fusion.5), channel_id=1, source_target_pairs={{4,0},{8,4},{12,8},{16,12},{20,16},{24,20},{28,24},{32,28},{36,32}... | collective-permute-start | bytes 786440 | tf_op jit(solution)/shard_map/while/body/eval_jaxpr/ppermute | solution.py:13
  501.0 11.1 %collective-permute-start.1 = (f32[4,128,128]{2,1,0:T(8,128)S(1)}, f32[4,128,128]{2,1,0:T(8,128)S(1)}, u32[]{:S(2)}, u32[]{:S(2)}) collective-permute-start(f32[4,128,128]{2,1,0:T(8,128)S(1)} %multiply_add_fusion.5), channel_id=1, source_target_pairs={{4,0},{8,4},{12,8},{16,12},{20,16},{24,20},{28,24},{32,28},{36,32}... | collective-permute-start | bytes 786440 | tf_op jit(solution)/shard_map/while/body/eval_jaxpr/ppermute | solution.py:13
  512.2 10.5 %collective-permute-start.1 = (f32[4,128,128]{2,1,0:T(8,128)S(1)}, f32[4,128,128]{2,1,0:T(8,128)S(1)}, u32[]{:S(2)}, u32[]{:S(2)}) collective-permute-start(f32[4,128,128]{2,1,0:T(8,128)S(1)} %multiply_add_fusion.5), channel_id=1, source_target_pairs={{4,0},{8,4},{12,8},{16,12},{20,16},{24,20},{28,24},{32,28},{36,32}... | collective-permute-start | bytes 786440 | tf_op jit(solution)/shard_map/while/body/eval_jaxpr/ppermute | solution.py:13
  522.8 10.0 collective-permute-start.1
  532.9 11.7 %collective-permute-start.1 = (f32[4,128,128]{2,1,0:T(8,128)S(1)}, f32[4,128,128]{2,1,0:T(8,128)S(1)}, u32[]{:S(2)}, u32[]{:S(2)}) collective-permute-start(f32[4,128,128]{2,1,0:T(8,128)S(1)} %multiply_add_fusion.5), channel_id=1, source_target_pairs={{4,0},{8,4},{12,8},{16,12},{20,16},{24,20},{28,24},{32,28},{36,32}... | collective-permute-start | bytes 786440 | tf_op jit(solution)/shard_map/while/body/eval_jaxpr/ppermute | solution.py:13
  544.6 11.9 %collective-permute-start.1 = (f32[4,128,128]{2,1,0:T(8,128)S(1)}, f32[4,128,128]{2,1,0:T(8,128)S(1)}, u32[]{:S(2)}, u32[]{:S(2)}) collective-permute-start(f32[4,128,128]{2,1,0:T(8,128)S(1)} %multiply_add_fusion.5), channel_id=1, source_target_pairs={{4,0},{8,4},{12,8},{16,12},{20,16},{24,20},{28,24},{32,28},{36,32}... | collective-permute-start | bytes 786440 | tf_op jit(solution)/shard_map/while/body/eval_jaxpr/ppermute | solution.py:13
  556.6 10.9 %collective-permute-start.1 = (f32[4,128,128]{2,1,0:T(8,128)S(1)}, f32[4,128,128]{2,1,0:T(8,128)S(1)}, u32[]{:S(2)}, u32[]{:S(2)}) collective-permute-start(f32[4,128,128]{2,1,0:T(8,128)S(1)} %multiply_add_fusion.5), channel_id=1, source_target_pairs={{4,0},{8,4},{12,8},{16,12},{20,16},{24,20},{28,24},{32,28},{36,32}... | collective-permute-start | bytes 786440 | tf_op jit(solution)/shard_map/while/body/eval_jaxpr/ppermute | solution.py:13
  567.6 9.4 collective-permute-start.1
  577.1 9.8 collective-permute-start.1
  587.1 10.9 %collective-permute-start.1 = (f32[4,128,128]{2,1,0:T(8,128)S(1)}, f32[4,128,128]{2,1,0:T(8,128)S(1)}, u32[]{:S(2)}, u32[]{:S(2)}) collective-permute-start(f32[4,128,128]{2,1,0:T(8,128)S(1)} %multiply_add_fusion.5), channel_id=1, source_target_pairs={{4,0},{8,4},{12,8},{16,12},{20,16},{24,20},{28,24},{32,28},{36,32}... | collective-permute-start | bytes 786440 | tf_op jit(solution)/shard_map/while/body/eval_jaxpr/ppermute | solution.py:13
  598.0 12.6 %collective-permute-start.1 = (f32[4,128,128]{2,1,0:T(8,128)S(1)}, f32[4,128,128]{2,1,0:T(8,128)S(1)}, u32[]{:S(2)}, u32[]{:S(2)}) collective-permute-start(f32[4,128,128]{2,1,0:T(8,128)S(1)} %multiply_add_fusion.5), channel_id=1, source_target_pairs={{4,0},{8,4},{12,8},{16,12},{20,16},{24,20},{28,24},{32,28},{36,32}... | collective-permute-start | bytes 786440 | tf_op jit(solution)/shard_map/while/body/eval_jaxpr/ppermute | solution.py:13
  610.7 10.6 %collective-permute-start.1 = (f32[4,128,128]{2,1,0:T(8,128)S(1)}, f32[4,128,128]{2,1,0:T(8,128)S(1)}, u32[]{:S(2)}, u32[]{:S(2)}) collective-permute-start(f32[4,128,128]{2,1,0:T(8,128)S(1)} %multiply_add_fusion.5), channel_id=1, source_target_pairs={{4,0},{8,4},{12,8},{16,12},{20,16},{24,20},{28,24},{32,28},{36,32}... | collective-permute-start | bytes 786440 | tf_op jit(solution)/shard_map/while/body/eval_jaxpr/ppermute | solution.py:13
  621.4 11.6 %collective-permute-start.1 = (f32[4,128,128]{2,1,0:T(8,128)S(1)}, f32[4,128,128]{2,1,0:T(8,128)S(1)}, u32[]{:S(2)}, u32[]{:S(2)}) collective-permute-start(f32[4,128,128]{2,1,0:T(8,128)S(1)} %multiply_add_fusion.5), channel_id=1, source_target_pairs={{4,0},{8,4},{12,8},{16,12},{20,16},{24,20},{28,24},{32,28},{36,32}... | collective-permute-start | bytes 786440 | tf_op jit(solution)/shard_map/while/body/eval_jaxpr/ppermute | solution.py:13
  633.1 17.4 %collective-permute-start.1 = (f32[4,128,128]{2,1,0:T(8,128)S(1)}, f32[4,128,128]{2,1,0:T(8,128)S(1)}, u32[]{:S(2)}, u32[]{:S(2)}) collective-permute-start(f32[4,128,128]{2,1,0:T(8,128)S(1)} %multiply_add_fusion.5), channel_id=1, source_target_pairs={{4,0},{8,4},{12,8},{16,12},{20,16},{24,20},{28,24},{32,28},{36,32}... | collective-permute-start | bytes 786440 | tf_op jit(solution)/shard_map/while/body/eval_jaxpr/ppermute | solution.py:13
  650.6 12.5 %collective-permute-start.1 = (f32[4,128,128]{2,1,0:T(8,128)S(1)}, f32[4,128,128]{2,1,0:T(8,128)S(1)}, u32[]{:S(2)}, u32[]{:S(2)}) collective-permute-start(f32[4,128,128]{2,1,0:T(8,128)S(1)} %multiply_add_fusion.5), channel_id=1, source_target_pairs={{4,0},{8,4},{12,8},{16,12},{20,16},{24,20},{28,24},{32,28},{36,32}... | collective-permute-start | bytes 786440 | tf_op jit(solution)/shard_map/while/body/eval_jaxpr/ppermute | solution.py:13
  663.2 14.0 %collective-permute-start.1 = (f32[4,128,128]{2,1,0:T(8,128)S(1)}, f32[4,128,128]{2,1,0:T(8,128)S(1)}, u32[]{:S(2)}, u32[]{:S(2)}) collective-permute-start(f32[4,128,128]{2,1,0:T(8,128)S(1)} %multiply_add_fusion.5), channel_id=1, source_target_pairs={{4,0},{8,4},{12,8},{16,12},{20,16},{24,20},{28,24},{32,28},{36,32}... | collective-permute-start | bytes 786440 | tf_op jit(solution)/shard_map/while/body/eval_jaxpr/ppermute | solution.py:13
  677.3 11.3 %collective-permute-start.1 = (f32[4,128,128]{2,1,0:T(8,128)S(1)}, f32[4,128,128]{2,1,0:T(8,128)S(1)}, u32[]{:S(2)}, u32[]{:S(2)}) collective-permute-start(f32[4,128,128]{2,1,0:T(8,128)S(1)} %multiply_add_fusion.5), channel_id=1, source_target_pairs={{4,0},{8,4},{12,8},{16,12},{20,16},{24,20},{28,24},{32,28},{36,32}... | collective-permute-start | bytes 786440 | tf_op jit(solution)/shard_map/while/body/eval_jaxpr/ppermute | solution.py:13
  688.7 9.7 collective-permute-start.1
  698.5 12.1 %collective-permute-start.1 = (f32[4,128,128]{2,1,0:T(8,128)S(1)}, f32[4,128,128]{2,1,0:T(8,128)S(1)}, u32[]{:S(2)}, u32[]{:S(2)}) collective-permute-start(f32[4,128,128]{2,1,0:T(8,128)S(1)} %multiply_add_fusion.5), channel_id=1, source_target_pairs={{4,0},{8,4},{12,8},{16,12},{20,16},{24,20},{28,24},{32,28},{36,32}... | collective-permute-start | bytes 786440 | tf_op jit(solution)/shard_map/while/body/eval_jaxpr/ppermute | solution.py:13
  710.6 11.7 %collective-permute-start.1 = (f32[4,128,128]{2,1,0:T(8,128)S(1)}, f32[4,128,128]{2,1,0:T(8,128)S(1)}, u32[]{:S(2)}, u32[]{:S(2)}) collective-permute-start(f32[4,128,128]{2,1,0:T(8,128)S(1)} %multiply_add_fusion.5), channel_id=1, source_target_pairs={{4,0},{8,4},{12,8},{16,12},{20,16},{24,20},{28,24},{32,28},{36,32}... | collective-permute-start | bytes 786440 | tf_op jit(solution)/shard_map/while/body/eval_jaxpr/ppermute | solution.py:13
  722.5 12.2 %collective-permute-start.1 = (f32[4,128,128]{2,1,0:T(8,128)S(1)}, f32[4,128,128]{2,1,0:T(8,128)S(1)}, u32[]{:S(2)}, u32[]{:S(2)}) collective-permute-start(f32[4,128,128]{2,1,0:T(8,128)S(1)} %multiply_add_fusion.5), channel_id=1, source_target_pairs={{4,0},{8,4},{12,8},{16,12},{20,16},{24,20},{28,24},{32,28},{36,32}... | collective-permute-start | bytes 786440 | tf_op jit(solution)/shard_map/while/body/eval_jaxpr/ppermute | solution.py:13
  734.8 10.9 %collective-permute-start.1 = (f32[4,128,128]{2,1,0:T(8,128)S(1)}, f32[4,128,128]{2,1,0:T(8,128)S(1)}, u32[]{:S(2)}, u32[]{:S(2)}) collective-permute-start(f32[4,128,128]{2,1,0:T(8,128)S(1)} %multiply_add_fusion.5), channel_id=1, source_target_pairs={{4,0},{8,4},{12,8},{16,12},{20,16},{24,20},{28,24},{32,28},{36,32}... | collective-permute-start | bytes 786440 | tf_op jit(solution)/shard_map/while/body/eval_jaxpr/ppermute | solution.py:13
  745.8 11.5 %collective-permute-start.1 = (f32[4,128,128]{2,1,0:T(8,128)S(1)}, f32[4,128,128]{2,1,0:T(8,128)S(1)}, u32[]{:S(2)}, u32[]{:S(2)}) collective-permute-start(f32[4,128,128]{2,1,0:T(8,128)S(1)} %multiply_add_fusion.5), channel_id=1, source_target_pairs={{4,0},{8,4},{12,8},{16,12},{20,16},{24,20},{28,24},{32,28},{36,32}... | collective-permute-start | bytes 786440 | tf_op jit(solution)/shard_map/while/body/eval_jaxpr/ppermute | solution.py:13
  757.4 12.5 %collective-permute-start.1 = (f32[4,128,128]{2,1,0:T(8,128)S(1)}, f32[4,128,128]{2,1,0:T(8,128)S(1)}, u32[]{:S(2)}, u32[]{:S(2)}) collective-permute-start(f32[4,128,128]{2,1,0:T(8,128)S(1)} %multiply_add_fusion.5), channel_id=1, source_target_pairs={{4,0},{8,4},{12,8},{16,12},{20,16},{24,20},{28,24},{32,28},{36,32}... | collective-permute-start | bytes 786440 | tf_op jit(solution)/shard_map/while/body/eval_jaxpr/ppermute | solution.py:13
  (33 other events, 172.8 us)
Sparse Core Ops, SparseCore 0:
  859.7 66.5 reduce-scatter.3
where the time goes:
time: 1010 us
  waiting for transfers between devices  522 us (52%)
  starting transfers between devices  232 us (23%)
  blocking collectives  75.7 us (7%)
  matrix products  65.1 us (6%)
  local copies, waits for them, and re-layouts  63.2 us (6%)
  other arithmetic  35.6 us (4%)
  between operations  14.2 us (1%)
    ppermute x62, waiting for transfers between devices, passed_along(): lax.ppermute(value, axis, [(source, source + steps) for source in range(f...  464 us
    ppermute x62, starting transfers between devices, passed_along(): lax.ppermute(value, axis, [(source, source + steps) for source in range(f...  232 us
    psum x1, blocking collectives, shards(): gain_total = lax.psum(gain_term, 'ctx')  75.7 us
    unnamed x2, waiting for transfers between devices  58.4 us
  transfers between devices with their start and end apart: 63, of which 63 were waited for; matrix products, arithmetic and copies ran while one was open for 1% of the time, Pallas kernels for 0%

commit v1 on v0

--- a/solution.py
+++ b/solution.py
@@ -125,7 +125,7 @@
 
     later_grad = lax.fori_loop(0, ctx_size - 1, relay_back, jnp.zeros_like(local_grad))
     grad_q, grad_k, grad_v, grad_a, gain_term = pullback((cot_float, later_grad))
-    gain_total = lax.psum(gain_term, "ctx")
+    gain_total = jnp.sum(lax.all_gather(gain_term, "ctx"), axis=0)
     grad_gain = lax.psum_scatter(gain_total, "dp", scatter_dimension=1, tiled=True)
     return (
         primal.astype(jnp.bfloat16)[None],

time: 1010 us -> 987 us (0.977)
  waiting for transfers between devices: 522 us -> 469 us
  blocking collectives: 75.7 us -> 101 us
    all_gather x0 -> x1, blocking collectives: none -> 101 us  [shards(): gain_total = jnp.sum(lax.all_gather(gain_term, 'ctx'), axis=0)]
    psum x1 -> x0, blocking collectives: 75.7 us -> none  [shards(): gain_total = lax.psum(gain_term, 'ctx')]
    unnamed x2, waiting for transfers between devices: 58.4 us -> 5.16 us
where the time goes in v1:
time: 987 us; the launch traced here: 983 us
  waiting for transfers between devices  469 us (48%)
  starting transfers between devices  232 us (24%)
  blocking collectives  101 us (10%)
  matrix products  65.1 us (7%)
  local copies, waits for them, and re-layouts  63.8 us (6%)
  other arithmetic  35.7 us (4%)
  between operations  14.2 us (1%)
    ppermute x62, waiting for transfers between devices, passed_along(): lax.ppermute(value, axis, [(source, source + steps) for source in range(f...  464 us
    ppermute x62, starting transfers between devices, passed_along(): lax.ppermute(value, axis, [(source, source + steps) for source in range(f...  232 us
    all_gather x1, blocking collectives, shards(): gain_total = jnp.sum(lax.all_gather(gain_term, 'ctx'), axis=0)  101 us
  transfers between devices with their start and end apart: 63, of which 63 were waited for; matrix products, arithmetic and copies ran while one was open for 1% of the time, Pallas kernels for 0%

profile of v1, /device:TPU:2, one launch (start us, length us, event | category | flops | bytes accessed | tf_op | source)
XLA Modules:
  0.0 982.8 jit_solution(14313330743203578885)
XLA Ops:
  37.1 336.8 %while.62 = (s32[]{:T(128)}, f32[4,128,128]{2,1,0:T(8,128)S(1)}, f32[4]{0:T(128)S(1)}, f32[4,128,128]{2,1,0:T(8,128)S(1)}, s32[]{:T(128)}) while((s32[]{:T(128)}, f32[4,128,128]{2,1,0:T(8,128)S(1)}, f32[4]{0:T(128)S(1)}, f32[4,128,128]{2,1,0:T(8,128)S(1)}, s32[]{:T(128)}) %tuple.140), condition=%wide.region_7.8_spmd, body=%wide.region_6.7_spmd.sunk | while | flops 131074 | bytes 1835125 | solution.py:103
  90.1 6.5 collective-permute-start
  100.6 6.9 collective-permute-start
  112.5 7.1 collective-permute-start
  119.7 6.2 collective-permute-done
  126.0 7.4 collective-permute-start
  133.4 6.0 collective-permute-done
  139.5 6.5 collective-permute-start
  160.6 6.5 collective-permute-start
  171.1 6.5 collective-permute-start
  181.5 6.5 collective-permute-start
  192.0 6.5 collective-permute-start
  202.7 6.8 collective-permute-start
  214.7 7.1 collective-permute-start
  221.9 6.3 collective-permute-done
  228.3 7.5 collective-permute-start
  235.8 5.8 collective-permute-done
  241.7 6.2 collective-permute-start
  262.2 6.5 collective-permute-start
  272.7 6.5 collective-permute-start
  283.1 6.5 collective-permute-start
  293.6 6.5 collective-permute-start
  304.5 6.8 collective-permute-start
  316.8 7.1 collective-permute-start
  323.9 6.5 collective-permute-done
  330.5 7.2 collective-permute-start
  343.4 6.2 collective-permute-start
  353.6 5.9 collective-permute-start
  363.5 6.5 collective-permute-start
  373.8 27.3 %while.64 = (s32[]{:T(128)}, f32[4,128,128]{2,1,0:T(8,128)S(1)}, bf16[2,512,4,128]{1,3,2,0:T(8,128)(2,1)}, f32[2,4,128,128]{3,2,1,0:T(8,128)}, f32[2,4,512]{2,1,...) while((s32[]{:T(128)}, f32[4,128,128]{2,1,0:T(8,128)S(1)}, ...), condition=%wide.region_13.14_spmd.clone, body=%wide.region_8.13_spmd.clone.sunk | while | flops 1352081408 | bytes 9343697 | solution.py:70
  404.3 365.5 %while.63 = (s32[]{:T(128)}, f32[4,128,128]{2,1,0:T(8,128)S(1)}, f32[4]{0:T(128)S(1)}, f32[4,128,128]{2,1,0:T(8,128)S(1)}, s32[]{:T(128)}) while((s32[]{:T(128)}, f32[4,128,128]{2,1,0:T(8,128)S(1)}, f32[4]{0:T(128)S(1)}, f32[4,128,128]{2,1,0:T(8,128)S(1)}, s32[]{:T(128)}) %tuple.160), condition=%wide.region_15.16_spmd, body=%wide.region_14.15_spmd.sunk | while | flops 131074 | bytes 1835125 | solution.py:126
  405.7 9.5 collective-permute-done.1
  416.7 9.5 collective-permute-done.1
  427.6 9.6 collective-permute-done.1
  438.6 11.9 %collective-permute-done.1 = f32[4,128,128]{2,1,0:T(8,128)S(1)} collective-permute-done((f32[4,128,128]{2,1,0:T(8,128)S(1)}, f32[4,128,128]{2,1,0:T(8,128)S(1)}, u32[]{:S(2)}, u32[]{:S(2)}) %collective-permute-start.1) | collective-permute-done | bytes 262176 | tf_op jit(solution)/shard_map/while/body/eval_jaxpr/ppermute | solution.py:13
  451.9 12.8 %collective-permute-done.1 = f32[4,128,128]{2,1,0:T(8,128)S(1)} collective-permute-done((f32[4,128,128]{2,1,0:T(8,128)S(1)}, f32[4,128,128]{2,1,0:T(8,128)S(1)}, u32[]{:S(2)}, u32[]{:S(2)}) %collective-permute-start.1) | collective-permute-done | bytes 262176 | tf_op jit(solution)/shard_map/while/body/eval_jaxpr/ppermute | solution.py:13
  466.1 11.3 %collective-permute-done.1 = f32[4,128,128]{2,1,0:T(8,128)S(1)} collective-permute-done((f32[4,128,128]{2,1,0:T(8,128)S(1)}, f32[4,128,128]{2,1,0:T(8,128)S(1)}, u32[]{:S(2)}, u32[]{:S(2)}) %collective-permute-start.1) | collective-permute-done | bytes 262176 | tf_op jit(solution)/shard_map/while/body/eval_jaxpr/ppermute | solution.py:13
  478.8 10.0 %collective-permute-done.1 = f32[4,128,128]{2,1,0:T(8,128)S(1)} collective-permute-done((f32[4,128,128]{2,1,0:T(8,128)S(1)}, f32[4,128,128]{2,1,0:T(8,128)S(1)}, u32[]{:S(2)}, u32[]{:S(2)}) %collective-permute-start.1) | collective-permute-done | bytes 262176 | tf_op jit(solution)/shard_map/while/body/eval_jaxpr/ppermute | solution.py:13
  490.3 10.6 %collective-permute-done.1 = f32[4,128,128]{2,1,0:T(8,128)S(1)} collective-permute-done((f32[4,128,128]{2,1,0:T(8,128)S(1)}, f32[4,128,128]{2,1,0:T(8,128)S(1)}, u32[]{:S(2)}, u32[]{:S(2)}) %collective-permute-start.1) | collective-permute-done | bytes 262176 | tf_op jit(solution)/shard_map/while/body/eval_jaxpr/ppermute | solution.py:13
  502.3 9.4 collective-permute-done.1
  513.1 9.1 collective-permute-done.1
  523.6 8.8 collective-permute-done.1
  533.8 9.6 collective-permute-done.1
  544.7 10.5 %collective-permute-done.1 = f32[4,128,128]{2,1,0:T(8,128)S(1)} collective-permute-done((f32[4,128,128]{2,1,0:T(8,128)S(1)}, f32[4,128,128]{2,1,0:T(8,128)S(1)}, u32[]{:S(2)}, u32[]{:S(2)}) %collective-permute-start.1) | collective-permute-done | bytes 262176 | tf_op jit(solution)/shard_map/while/body/eval_jaxpr/ppermute | solution.py:13
  556.6 10.0 %collective-permute-done.1 = f32[4,128,128]{2,1,0:T(8,128)S(1)} collective-permute-done((f32[4,128,128]{2,1,0:T(8,128)S(1)}, f32[4,128,128]{2,1,0:T(8,128)S(1)}, u32[]{:S(2)}, u32[]{:S(2)}) %collective-permute-start.1) | collective-permute-done | bytes 262176 | tf_op jit(solution)/shard_map/while/body/eval_jaxpr/ppermute | solution.py:13
  568.0 8.2 collective-permute-done.1
  577.7 8.4 collective-permute-done.1
  587.5 10.4 %collective-permute-done.1 = f32[4,128,128]{2,1,0:T(8,128)S(1)} collective-permute-done((f32[4,128,128]{2,1,0:T(8,128)S(1)}, f32[4,128,128]{2,1,0:T(8,128)S(1)}, u32[]{:S(2)}, u32[]{:S(2)}) %collective-permute-start.1) | collective-permute-done | bytes 262176 | tf_op jit(solution)/shard_map/while/body/eval_jaxpr/ppermute | solution.py:13
  599.3 11.3 %collective-permute-done.1 = f32[4,128,128]{2,1,0:T(8,128)S(1)} collective-permute-done((f32[4,128,128]{2,1,0:T(8,128)S(1)}, f32[4,128,128]{2,1,0:T(8,128)S(1)}, u32[]{:S(2)}, u32[]{:S(2)}) %collective-permute-start.1) | collective-permute-done | bytes 262176 | tf_op jit(solution)/shard_map/while/body/eval_jaxpr/ppermute | solution.py:13
  612.0 9.3 collective-permute-done.1
  622.7 10.2 %collective-permute-done.1 = f32[4,128,128]{2,1,0:T(8,128)S(1)} collective-permute-done((f32[4,128,128]{2,1,0:T(8,128)S(1)}, f32[4,128,128]{2,1,0:T(8,128)S(1)}, u32[]{:S(2)}, u32[]{:S(2)}) %collective-permute-start.1) | collective-permute-done | bytes 262176 | tf_op jit(solution)/shard_map/while/body/eval_jaxpr/ppermute | solution.py:13
  634.4 16.1 %collective-permute-done.1 = f32[4,128,128]{2,1,0:T(8,128)S(1)} collective-permute-done((f32[4,128,128]{2,1,0:T(8,128)S(1)}, f32[4,128,128]{2,1,0:T(8,128)S(1)}, u32[]{:S(2)}, u32[]{:S(2)}) %collective-permute-start.1) | collective-permute-done | bytes 262176 | tf_op jit(solution)/shard_map/while/body/eval_jaxpr/ppermute | solution.py:13
  651.9 11.2 %collective-permute-done.1 = f32[4,128,128]{2,1,0:T(8,128)S(1)} collective-permute-done((f32[4,128,128]{2,1,0:T(8,128)S(1)}, f32[4,128,128]{2,1,0:T(8,128)S(1)}, u32[]{:S(2)}, u32[]{:S(2)}) %collective-permute-start.1) | collective-permute-done | bytes 262176 | tf_op jit(solution)/shard_map/while/body/eval_jaxpr/ppermute | solution.py:13
  664.5 12.7 %collective-permute-done.1 = f32[4,128,128]{2,1,0:T(8,128)S(1)} collective-permute-done((f32[4,128,128]{2,1,0:T(8,128)S(1)}, f32[4,128,128]{2,1,0:T(8,128)S(1)}, u32[]{:S(2)}, u32[]{:S(2)}) %collective-permute-start.1) | collective-permute-done | bytes 262176 | tf_op jit(solution)/shard_map/while/body/eval_jaxpr/ppermute | solution.py:13
  678.6 10.0 %collective-permute-done.1 = f32[4,128,128]{2,1,0:T(8,128)S(1)} collective-permute-done((f32[4,128,128]{2,1,0:T(8,128)S(1)}, f32[4,128,128]{2,1,0:T(8,128)S(1)}, u32[]{:S(2)}, u32[]{:S(2)}) %collective-permute-start.1) | collective-permute-done | bytes 262176 | tf_op jit(solution)/shard_map/while/body/eval_jaxpr/ppermute | solution.py:13
  690.0 8.4 collective-permute-done.1
  699.8 10.7 %collective-permute-done.1 = f32[4,128,128]{2,1,0:T(8,128)S(1)} collective-permute-done((f32[4,128,128]{2,1,0:T(8,128)S(1)}, f32[4,128,128]{2,1,0:T(8,128)S(1)}, u32[]{:S(2)}, u32[]{:S(2)}) %collective-permute-start.1) | collective-permute-done | bytes 262176 | tf_op jit(solution)/shard_map/while/body/eval_jaxpr/ppermute | solution.py:13
  711.9 10.4 %collective-permute-done.1 = f32[4,128,128]{2,1,0:T(8,128)S(1)} collective-permute-done((f32[4,128,128]{2,1,0:T(8,128)S(1)}, f32[4,128,128]{2,1,0:T(8,128)S(1)}, u32[]{:S(2)}, u32[]{:S(2)}) %collective-permute-start.1) | collective-permute-done | bytes 262176 | tf_op jit(solution)/shard_map/while/body/eval_jaxpr/ppermute | solution.py:13
  723.8 10.9 %collective-permute-done.1 = f32[4,128,128]{2,1,0:T(8,128)S(1)} collective-permute-done((f32[4,128,128]{2,1,0:T(8,128)S(1)}, f32[4,128,128]{2,1,0:T(8,128)S(1)}, u32[]{:S(2)}, u32[]{:S(2)}) %collective-permute-start.1) | collective-permute-done | bytes 262176 | tf_op jit(solution)/shard_map/while/body/eval_jaxpr/ppermute | solution.py:13
  736.1 9.6 collective-permute-done.1
  747.1 10.2 %collective-permute-done.1 = f32[4,128,128]{2,1,0:T(8,128)S(1)} collective-permute-done((f32[4,128,128]{2,1,0:T(8,128)S(1)}, f32[4,128,128]{2,1,0:T(8,128)S(1)}, u32[]{:S(2)}, u32[]{:S(2)}) %collective-permute-start.1) | collective-permute-done | bytes 262176 | tf_op jit(solution)/shard_map/while/body/eval_jaxpr/ppermute | solution.py:13
  758.7 11.2 %collective-permute-done.1 = f32[4,128,128]{2,1,0:T(8,128)S(1)} collective-permute-done((f32[4,128,128]{2,1,0:T(8,128)S(1)}, f32[4,128,128]{2,1,0:T(8,128)S(1)}, u32[]{:S(2)}, u32[]{:S(2)}) %collective-permute-start.1) | collective-permute-done | bytes 262176 | tf_op jit(solution)/shard_map/while/body/eval_jaxpr/ppermute | solution.py:13
  773.6 85.2 %while.65 = (s32[]{:T(128)}, f32[4,128]{1,0:T(4,128)S(1)}, f32[4,128,128]{2,1,0:T(8,128)S(1)}, bf16[2,512,4,128]{3,2,1,0:T(4,128)(2,1)}, bf16[2,512,4,128]{3,2,1...) while((s32[]{:T(128)}, f32[4,128]{1,0:T(4,128)S(1)}, ...), condition=%wide.region_30.31_spmd.clone, body=%wide.region_16.30_spmd.clone.sunk | while | flops 3394863616 | bytes 116524784 | solution.py:70
  858.8 101.5 %all-gather.1 = f32[32,4,128]{2,1,0:T(4,128)S(1)} all-gather(f32[1,4,128]{2,1,0:T(4,128)S(1)} %bitcast.364), channel_id=2, replica_groups=mesh['dp'=2,'ctx'=32,'head'=4] {'ctx'}, dimensions={0}, use_global_device_ids=true | all-gather | bytes 67584 | tf_op jit(solution)/shard_map/all_gather | solution.py:128
  (407 shorter events, 358.7 us)
Async XLA Ops:
  7.2 967.4 %reduce-scatter.4.cloned.1.call-start = ((), (), s32[]{:S(2)}) async-start(), calls=%async_computation.1 | async-start | bytes 98304
  37.2 9.0 collective-permute-start
  46.3 9.1 collective-permute-start
  55.5 8.3 collective-permute-start
  63.8 8.3 collective-permute-start
  72.2 8.3 collective-permute-start
  80.5 9.5 collective-permute-start
  90.1 10.4 %collective-permute-start = (f32[4,128,128]{2,1,0:T(8,128)S(1)}, f32[4,128,128]{2,1,0:T(8,128)S(1)}, u32[]{:S(2)}, u32[]{:S(2)}) collective-permute-start(f32[4,128,128]{2,1,0:T(8,128)S(1)} %multiply_add_fusion.4), channel_id=1, source_target_pairs={{0,4},{4,8},{8,12},{12,16},{16,20},{20,24},{24,28},{28,32},{32,36}... | collective-permute-start | bytes 786440 | tf_op jit(solution)/shard_map/while/body/eval_jaxpr/ppermute | solution.py:13
  100.6 11.9 %collective-permute-start = (f32[4,128,128]{2,1,0:T(8,128)S(1)}, f32[4,128,128]{2,1,0:T(8,128)S(1)}, u32[]{:S(2)}, u32[]{:S(2)}) collective-permute-start(f32[4,128,128]{2,1,0:T(8,128)S(1)} %multiply_add_fusion.4), channel_id=1, source_target_pairs={{0,4},{4,8},{8,12},{12,16},{16,20},{20,24},{24,28},{28,32},{32,36}... | collective-permute-start | bytes 786440 | tf_op jit(solution)/shard_map/while/body/eval_jaxpr/ppermute | solution.py:13
  112.5 13.4 %collective-permute-start = (f32[4,128,128]{2,1,0:T(8,128)S(1)}, f32[4,128,128]{2,1,0:T(8,128)S(1)}, u32[]{:S(2)}, u32[]{:S(2)}) collective-permute-start(f32[4,128,128]{2,1,0:T(8,128)S(1)} %multiply_add_fusion.4), channel_id=1, source_target_pairs={{0,4},{4,8},{8,12},{12,16},{16,20},{20,24},{24,28},{28,32},{32,36}... | collective-permute-start | bytes 786440 | tf_op jit(solution)/shard_map/while/body/eval_jaxpr/ppermute | solution.py:13
  126.0 13.4 %collective-permute-start = (f32[4,128,128]{2,1,0:T(8,128)S(1)}, f32[4,128,128]{2,1,0:T(8,128)S(1)}, u32[]{:S(2)}, u32[]{:S(2)}) collective-permute-start(f32[4,128,128]{2,1,0:T(8,128)S(1)} %multiply_add_fusion.4), channel_id=1, source_target_pairs={{0,4},{4,8},{8,12},{12,16},{16,20},{20,24},{24,28},{28,32},{32,36}... | collective-permute-start | bytes 786440 | tf_op jit(solution)/shard_map/while/body/eval_jaxpr/ppermute | solution.py:13
  139.5 11.2 %collective-permute-start = (f32[4,128,128]{2,1,0:T(8,128)S(1)}, f32[4,128,128]{2,1,0:T(8,128)S(1)}, u32[]{:S(2)}, u32[]{:S(2)}) collective-permute-start(f32[4,128,128]{2,1,0:T(8,128)S(1)} %multiply_add_fusion.4), channel_id=1, source_target_pairs={{0,4},{4,8},{8,12},{12,16},{16,20},{20,24},{24,28},{28,32},{32,36}... | collective-permute-start | bytes 786440 | tf_op jit(solution)/shard_map/while/body/eval_jaxpr/ppermute | solution.py:13
  150.9 9.6 collective-permute-start
  160.6 10.4 %collective-permute-start = (f32[4,128,128]{2,1,0:T(8,128)S(1)}, f32[4,128,128]{2,1,0:T(8,128)S(1)}, u32[]{:S(2)}, u32[]{:S(2)}) collective-permute-start(f32[4,128,128]{2,1,0:T(8,128)S(1)} %multiply_add_fusion.4), channel_id=1, source_target_pairs={{0,4},{4,8},{8,12},{12,16},{16,20},{20,24},{24,28},{28,32},{32,36}... | collective-permute-start | bytes 786440 | tf_op jit(solution)/shard_map/while/body/eval_jaxpr/ppermute | solution.py:13
  171.1 10.4 %collective-permute-start = (f32[4,128,128]{2,1,0:T(8,128)S(1)}, f32[4,128,128]{2,1,0:T(8,128)S(1)}, u32[]{:S(2)}, u32[]{:S(2)}) collective-permute-start(f32[4,128,128]{2,1,0:T(8,128)S(1)} %multiply_add_fusion.4), channel_id=1, source_target_pairs={{0,4},{4,8},{8,12},{12,16},{16,20},{20,24},{24,28},{28,32},{32,36}... | collective-permute-start | bytes 786440 | tf_op jit(solution)/shard_map/while/body/eval_jaxpr/ppermute | solution.py:13
  181.5 10.4 %collective-permute-start = (f32[4,128,128]{2,1,0:T(8,128)S(1)}, f32[4,128,128]{2,1,0:T(8,128)S(1)}, u32[]{:S(2)}, u32[]{:S(2)}) collective-permute-start(f32[4,128,128]{2,1,0:T(8,128)S(1)} %multiply_add_fusion.4), channel_id=1, source_target_pairs={{0,4},{4,8},{8,12},{12,16},{16,20},{20,24},{24,28},{28,32},{32,36}... | collective-permute-start | bytes 786440 | tf_op jit(solution)/shard_map/while/body/eval_jaxpr/ppermute | solution.py:13
  192.0 10.6 %collective-permute-start = (f32[4,128,128]{2,1,0:T(8,128)S(1)}, f32[4,128,128]{2,1,0:T(8,128)S(1)}, u32[]{:S(2)}, u32[]{:S(2)}) collective-permute-start(f32[4,128,128]{2,1,0:T(8,128)S(1)} %multiply_add_fusion.4), channel_id=1, source_target_pairs={{0,4},{4,8},{8,12},{12,16},{16,20},{20,24},{24,28},{28,32},{32,36}... | collective-permute-start | bytes 786440 | tf_op jit(solution)/shard_map/while/body/eval_jaxpr/ppermute | solution.py:13
  202.7 11.9 %collective-permute-start = (f32[4,128,128]{2,1,0:T(8,128)S(1)}, f32[4,128,128]{2,1,0:T(8,128)S(1)}, u32[]{:S(2)}, u32[]{:S(2)}) collective-permute-start(f32[4,128,128]{2,1,0:T(8,128)S(1)} %multiply_add_fusion.4), channel_id=1, source_target_pairs={{0,4},{4,8},{8,12},{12,16},{16,20},{20,24},{24,28},{28,32},{32,36}... | collective-permute-start | bytes 786440 | tf_op jit(solution)/shard_map/while/body/eval_jaxpr/ppermute | solution.py:13
  214.7 13.5 %collective-permute-start = (f32[4,128,128]{2,1,0:T(8,128)S(1)}, f32[4,128,128]{2,1,0:T(8,128)S(1)}, u32[]{:S(2)}, u32[]{:S(2)}) collective-permute-start(f32[4,128,128]{2,1,0:T(8,128)S(1)} %multiply_add_fusion.4), channel_id=1, source_target_pairs={{0,4},{4,8},{8,12},{12,16},{16,20},{20,24},{24,28},{28,32},{32,36}... | collective-permute-start | bytes 786440 | tf_op jit(solution)/shard_map/while/body/eval_jaxpr/ppermute | solution.py:13
  228.3 13.3 %collective-permute-start = (f32[4,128,128]{2,1,0:T(8,128)S(1)}, f32[4,128,128]{2,1,0:T(8,128)S(1)}, u32[]{:S(2)}, u32[]{:S(2)}) collective-permute-start(f32[4,128,128]{2,1,0:T(8,128)S(1)} %multiply_add_fusion.4), channel_id=1, source_target_pairs={{0,4},{4,8},{8,12},{12,16},{16,20},{20,24},{24,28},{28,32},{32,36}... | collective-permute-start | bytes 786440 | tf_op jit(solution)/shard_map/while/body/eval_jaxpr/ppermute | solution.py:13
  241.7 10.8 %collective-permute-start = (f32[4,128,128]{2,1,0:T(8,128)S(1)}, f32[4,128,128]{2,1,0:T(8,128)S(1)}, u32[]{:S(2)}, u32[]{:S(2)}) collective-permute-start(f32[4,128,128]{2,1,0:T(8,128)S(1)} %multiply_add_fusion.4), channel_id=1, source_target_pairs={{0,4},{4,8},{8,12},{12,16},{16,20},{20,24},{24,28},{28,32},{32,36}... | collective-permute-start | bytes 786440 | tf_op jit(solution)/shard_map/while/body/eval_jaxpr/ppermute | solution.py:13
  252.6 9.6 collective-permute-start
  262.2 10.4 %collective-permute-start = (f32[4,128,128]{2,1,0:T(8,128)S(1)}, f32[4,128,128]{2,1,0:T(8,128)S(1)}, u32[]{:S(2)}, u32[]{:S(2)}) collective-permute-start(f32[4,128,128]{2,1,0:T(8,128)S(1)} %multiply_add_fusion.4), channel_id=1, source_target_pairs={{0,4},{4,8},{8,12},{12,16},{16,20},{20,24},{24,28},{28,32},{32,36}... | collective-permute-start | bytes 786440 | tf_op jit(solution)/shard_map/while/body/eval_jaxpr/ppermute | solution.py:13
  272.7 10.4 %collective-permute-start = (f32[4,128,128]{2,1,0:T(8,128)S(1)}, f32[4,128,128]{2,1,0:T(8,128)S(1)}, u32[]{:S(2)}, u32[]{:S(2)}) collective-permute-start(f32[4,128,128]{2,1,0:T(8,128)S(1)} %multiply_add_fusion.4), channel_id=1, source_target_pairs={{0,4},{4,8},{8,12},{12,16},{16,20},{20,24},{24,28},{28,32},{32,36}... | collective-permute-start | bytes 786440 | tf_op jit(solution)/shard_map/while/body/eval_jaxpr/ppermute | solution.py:13
  283.1 10.4 %collective-permute-start = (f32[4,128,128]{2,1,0:T(8,128)S(1)}, f32[4,128,128]{2,1,0:T(8,128)S(1)}, u32[]{:S(2)}, u32[]{:S(2)}) collective-permute-start(f32[4,128,128]{2,1,0:T(8,128)S(1)} %multiply_add_fusion.4), channel_id=1, source_target_pairs={{0,4},{4,8},{8,12},{12,16},{16,20},{20,24},{24,28},{28,32},{32,36}... | collective-permute-start | bytes 786440 | tf_op jit(solution)/shard_map/while/body/eval_jaxpr/ppermute | solution.py:13
  293.6 10.8 %collective-permute-start = (f32[4,128,128]{2,1,0:T(8,128)S(1)}, f32[4,128,128]{2,1,0:T(8,128)S(1)}, u32[]{:S(2)}, u32[]{:S(2)}) collective-permute-start(f32[4,128,128]{2,1,0:T(8,128)S(1)} %multiply_add_fusion.4), channel_id=1, source_target_pairs={{0,4},{4,8},{8,12},{12,16},{16,20},{20,24},{24,28},{28,32},{32,36}... | collective-permute-start | bytes 786440 | tf_op jit(solution)/shard_map/while/body/eval_jaxpr/ppermute | solution.py:13
  304.5 12.2 %collective-permute-start = (f32[4,128,128]{2,1,0:T(8,128)S(1)}, f32[4,128,128]{2,1,0:T(8,128)S(1)}, u32[]{:S(2)}, u32[]{:S(2)}) collective-permute-start(f32[4,128,128]{2,1,0:T(8,128)S(1)} %multiply_add_fusion.4), channel_id=1, source_target_pairs={{0,4},{4,8},{8,12},{12,16},{16,20},{20,24},{24,28},{28,32},{32,36}... | collective-permute-start | bytes 786440 | tf_op jit(solution)/shard_map/while/body/eval_jaxpr/ppermute | solution.py:13
  316.8 13.6 %collective-permute-start = (f32[4,128,128]{2,1,0:T(8,128)S(1)}, f32[4,128,128]{2,1,0:T(8,128)S(1)}, u32[]{:S(2)}, u32[]{:S(2)}) collective-permute-start(f32[4,128,128]{2,1,0:T(8,128)S(1)} %multiply_add_fusion.4), channel_id=1, source_target_pairs={{0,4},{4,8},{8,12},{12,16},{16,20},{20,24},{24,28},{28,32},{32,36}... | collective-permute-start | bytes 786440 | tf_op jit(solution)/shard_map/while/body/eval_jaxpr/ppermute | solution.py:13
  330.5 12.8 %collective-permute-start = (f32[4,128,128]{2,1,0:T(8,128)S(1)}, f32[4,128,128]{2,1,0:T(8,128)S(1)}, u32[]{:S(2)}, u32[]{:S(2)}) collective-permute-start(f32[4,128,128]{2,1,0:T(8,128)S(1)} %multiply_add_fusion.4), channel_id=1, source_target_pairs={{0,4},{4,8},{8,12},{12,16},{16,20},{20,24},{24,28},{28,32},{32,36}... | collective-permute-start | bytes 786440 | tf_op jit(solution)/shard_map/while/body/eval_jaxpr/ppermute | solution.py:13
  343.4 10.1 %collective-permute-start = (f32[4,128,128]{2,1,0:T(8,128)S(1)}, f32[4,128,128]{2,1,0:T(8,128)S(1)}, u32[]{:S(2)}, u32[]{:S(2)}) collective-permute-start(f32[4,128,128]{2,1,0:T(8,128)S(1)} %multiply_add_fusion.4), channel_id=1, source_target_pairs={{0,4},{4,8},{8,12},{12,16},{16,20},{20,24},{24,28},{28,32},{32,36}... | collective-permute-start | bytes 786440 | tf_op jit(solution)/shard_map/while/body/eval_jaxpr/ppermute | solution.py:13
  353.6 9.7 collective-permute-start
  363.5 10.4 %collective-permute-start = (f32[4,128,128]{2,1,0:T(8,128)S(1)}, f32[4,128,128]{2,1,0:T(8,128)S(1)}, u32[]{:S(2)}, u32[]{:S(2)}) collective-permute-start(f32[4,128,128]{2,1,0:T(8,128)S(1)} %multiply_add_fusion.4), channel_id=1, source_target_pairs={{0,4},{4,8},{8,12},{12,16},{16,20},{20,24},{24,28},{28,32},{32,36}... | collective-permute-start | bytes 786440 | tf_op jit(solution)/shard_map/while/body/eval_jaxpr/ppermute | solution.py:13
  404.4 10.8 %collective-permute-start.1 = (f32[4,128,128]{2,1,0:T(8,128)S(1)}, f32[4,128,128]{2,1,0:T(8,128)S(1)}, u32[]{:S(2)}, u32[]{:S(2)}) collective-permute-start(f32[4,128,128]{2,1,0:T(8,128)S(1)} %multiply_add_fusion.5), channel_id=1, source_target_pairs={{4,0},{8,4},{12,8},{16,12},{20,16},{24,20},{28,24},{32,28},{36,32}... | collective-permute-start | bytes 786440 | tf_op jit(solution)/shard_map/while/body/eval_jaxpr/ppermute | solution.py:13
  415.3 10.8 %collective-permute-start.1 = (f32[4,128,128]{2,1,0:T(8,128)S(1)}, f32[4,128,128]{2,1,0:T(8,128)S(1)}, u32[]{:S(2)}, u32[]{:S(2)}) collective-permute-start(f32[4,128,128]{2,1,0:T(8,128)S(1)} %multiply_add_fusion.5), channel_id=1, source_target_pairs={{4,0},{8,4},{12,8},{16,12},{20,16},{24,20},{28,24},{32,28},{36,32}... | collective-permute-start | bytes 786440 | tf_op jit(solution)/shard_map/while/body/eval_jaxpr/ppermute | solution.py:13
  426.3 11.0 %collective-permute-start.1 = (f32[4,128,128]{2,1,0:T(8,128)S(1)}, f32[4,128,128]{2,1,0:T(8,128)S(1)}, u32[]{:S(2)}, u32[]{:S(2)}) collective-permute-start(f32[4,128,128]{2,1,0:T(8,128)S(1)} %multiply_add_fusion.5), channel_id=1, source_target_pairs={{4,0},{8,4},{12,8},{16,12},{20,16},{24,20},{28,24},{32,28},{36,32}... | collective-permute-start | bytes 786440 | tf_op jit(solution)/shard_map/while/body/eval_jaxpr/ppermute | solution.py:13
  437.3 13.2 %collective-permute-start.1 = (f32[4,128,128]{2,1,0:T(8,128)S(1)}, f32[4,128,128]{2,1,0:T(8,128)S(1)}, u32[]{:S(2)}, u32[]{:S(2)}) collective-permute-start(f32[4,128,128]{2,1,0:T(8,128)S(1)} %multiply_add_fusion.5), channel_id=1, source_target_pairs={{4,0},{8,4},{12,8},{16,12},{20,16},{24,20},{28,24},{32,28},{36,32}... | collective-permute-start | bytes 786440 | tf_op jit(solution)/shard_map/while/body/eval_jaxpr/ppermute | solution.py:13
  450.6 14.1 %collective-permute-start.1 = (f32[4,128,128]{2,1,0:T(8,128)S(1)}, f32[4,128,128]{2,1,0:T(8,128)S(1)}, u32[]{:S(2)}, u32[]{:S(2)}) collective-permute-start(f32[4,128,128]{2,1,0:T(8,128)S(1)} %multiply_add_fusion.5), channel_id=1, source_target_pairs={{4,0},{8,4},{12,8},{16,12},{20,16},{24,20},{28,24},{32,28},{36,32}... | collective-permute-start | bytes 786440 | tf_op jit(solution)/shard_map/while/body/eval_jaxpr/ppermute | solution.py:13
  464.8 12.6 %collective-permute-start.1 = (f32[4,128,128]{2,1,0:T(8,128)S(1)}, f32[4,128,128]{2,1,0:T(8,128)S(1)}, u32[]{:S(2)}, u32[]{:S(2)}) collective-permute-start(f32[4,128,128]{2,1,0:T(8,128)S(1)} %multiply_add_fusion.5), channel_id=1, source_target_pairs={{4,0},{8,4},{12,8},{16,12},{20,16},{24,20},{28,24},{32,28},{36,32}... | collective-permute-start | bytes 786440 | tf_op jit(solution)/shard_map/while/body/eval_jaxpr/ppermute | solution.py:13
  477.5 11.3 %collective-permute-start.1 = (f32[4,128,128]{2,1,0:T(8,128)S(1)}, f32[4,128,128]{2,1,0:T(8,128)S(1)}, u32[]{:S(2)}, u32[]{:S(2)}) collective-permute-start(f32[4,128,128]{2,1,0:T(8,128)S(1)} %multiply_add_fusion.5), channel_id=1, source_target_pairs={{4,0},{8,4},{12,8},{16,12},{20,16},{24,20},{28,24},{32,28},{36,32}... | collective-permute-start | bytes 786440 | tf_op jit(solution)/shard_map/while/body/eval_jaxpr/ppermute | solution.py:13
  489.0 12.0 %collective-permute-start.1 = (f32[4,128,128]{2,1,0:T(8,128)S(1)}, f32[4,128,128]{2,1,0:T(8,128)S(1)}, u32[]{:S(2)}, u32[]{:S(2)}) collective-permute-start(f32[4,128,128]{2,1,0:T(8,128)S(1)} %multiply_add_fusion.5), channel_id=1, source_target_pairs={{4,0},{8,4},{12,8},{16,12},{20,16},{24,20},{28,24},{32,28},{36,32}... | collective-permute-start | bytes 786440 | tf_op jit(solution)/shard_map/while/body/eval_jaxpr/ppermute | solution.py:13
  501.0 10.7 %collective-permute-start.1 = (f32[4,128,128]{2,1,0:T(8,128)S(1)}, f32[4,128,128]{2,1,0:T(8,128)S(1)}, u32[]{:S(2)}, u32[]{:S(2)}) collective-permute-start(f32[4,128,128]{2,1,0:T(8,128)S(1)} %multiply_add_fusion.5), channel_id=1, source_target_pairs={{4,0},{8,4},{12,8},{16,12},{20,16},{24,20},{28,24},{32,28},{36,32}... | collective-permute-start | bytes 786440 | tf_op jit(solution)/shard_map/while/body/eval_jaxpr/ppermute | solution.py:13
  511.8 10.4 %collective-permute-start.1 = (f32[4,128,128]{2,1,0:T(8,128)S(1)}, f32[4,128,128]{2,1,0:T(8,128)S(1)}, u32[]{:S(2)}, u32[]{:S(2)}) collective-permute-start(f32[4,128,128]{2,1,0:T(8,128)S(1)} %multiply_add_fusion.5), channel_id=1, source_target_pairs={{4,0},{8,4},{12,8},{16,12},{20,16},{24,20},{28,24},{32,28},{36,32}... | collective-permute-start | bytes 786440 | tf_op jit(solution)/shard_map/while/body/eval_jaxpr/ppermute | solution.py:13
  522.2 10.1 %collective-permute-start.1 = (f32[4,128,128]{2,1,0:T(8,128)S(1)}, f32[4,128,128]{2,1,0:T(8,128)S(1)}, u32[]{:S(2)}, u32[]{:S(2)}) collective-permute-start(f32[4,128,128]{2,1,0:T(8,128)S(1)} %multiply_add_fusion.5), channel_id=1, source_target_pairs={{4,0},{8,4},{12,8},{16,12},{20,16},{24,20},{28,24},{32,28},{36,32}... | collective-permute-start | bytes 786440 | tf_op jit(solution)/shard_map/while/body/eval_jaxpr/ppermute | solution.py:13
  532.5 10.9 %collective-permute-start.1 = (f32[4,128,128]{2,1,0:T(8,128)S(1)}, f32[4,128,128]{2,1,0:T(8,128)S(1)}, u32[]{:S(2)}, u32[]{:S(2)}) collective-permute-start(f32[4,128,128]{2,1,0:T(8,128)S(1)} %multiply_add_fusion.5), channel_id=1, source_target_pairs={{4,0},{8,4},{12,8},{16,12},{20,16},{24,20},{28,24},{32,28},{36,32}... | collective-permute-start | bytes 786440 | tf_op jit(solution)/shard_map/while/body/eval_jaxpr/ppermute | solution.py:13
  543.4 11.8 %collective-permute-start.1 = (f32[4,128,128]{2,1,0:T(8,128)S(1)}, f32[4,128,128]{2,1,0:T(8,128)S(1)}, u32[]{:S(2)}, u32[]{:S(2)}) collective-permute-start(f32[4,128,128]{2,1,0:T(8,128)S(1)} %multiply_add_fusion.5), channel_id=1, source_target_pairs={{4,0},{8,4},{12,8},{16,12},{20,16},{24,20},{28,24},{32,28},{36,32}... | collective-permute-start | bytes 786440 | tf_op jit(solution)/shard_map/while/body/eval_jaxpr/ppermute | solution.py:13
  555.3 11.3 %collective-permute-start.1 = (f32[4,128,128]{2,1,0:T(8,128)S(1)}, f32[4,128,128]{2,1,0:T(8,128)S(1)}, u32[]{:S(2)}, u32[]{:S(2)}) collective-permute-start(f32[4,128,128]{2,1,0:T(8,128)S(1)} %multiply_add_fusion.5), channel_id=1, source_target_pairs={{4,0},{8,4},{12,8},{16,12},{20,16},{24,20},{28,24},{32,28},{36,32}... | collective-permute-start | bytes 786440 | tf_op jit(solution)/shard_map/while/body/eval_jaxpr/ppermute | solution.py:13
  566.7 9.5 collective-permute-start.1
  576.4 9.7 collective-permute-start.1
  586.2 11.8 %collective-permute-start.1 = (f32[4,128,128]{2,1,0:T(8,128)S(1)}, f32[4,128,128]{2,1,0:T(8,128)S(1)}, u32[]{:S(2)}, u32[]{:S(2)}) collective-permute-start(f32[4,128,128]{2,1,0:T(8,128)S(1)} %multiply_add_fusion.5), channel_id=1, source_target_pairs={{4,0},{8,4},{12,8},{16,12},{20,16},{24,20},{28,24},{32,28},{36,32}... | collective-permute-start | bytes 786440 | tf_op jit(solution)/shard_map/while/body/eval_jaxpr/ppermute | solution.py:13
  598.0 12.6 %collective-permute-start.1 = (f32[4,128,128]{2,1,0:T(8,128)S(1)}, f32[4,128,128]{2,1,0:T(8,128)S(1)}, u32[]{:S(2)}, u32[]{:S(2)}) collective-permute-start(f32[4,128,128]{2,1,0:T(8,128)S(1)} %multiply_add_fusion.5), channel_id=1, source_target_pairs={{4,0},{8,4},{12,8},{16,12},{20,16},{24,20},{28,24},{32,28},{36,32}... | collective-permute-start | bytes 786440 | tf_op jit(solution)/shard_map/while/body/eval_jaxpr/ppermute | solution.py:13
  610.7 10.6 %collective-permute-start.1 = (f32[4,128,128]{2,1,0:T(8,128)S(1)}, f32[4,128,128]{2,1,0:T(8,128)S(1)}, u32[]{:S(2)}, u32[]{:S(2)}) collective-permute-start(f32[4,128,128]{2,1,0:T(8,128)S(1)} %multiply_add_fusion.5), channel_id=1, source_target_pairs={{4,0},{8,4},{12,8},{16,12},{20,16},{24,20},{28,24},{32,28},{36,32}... | collective-permute-start | bytes 786440 | tf_op jit(solution)/shard_map/while/body/eval_jaxpr/ppermute | solution.py:13
  621.4 11.6 %collective-permute-start.1 = (f32[4,128,128]{2,1,0:T(8,128)S(1)}, f32[4,128,128]{2,1,0:T(8,128)S(1)}, u32[]{:S(2)}, u32[]{:S(2)}) collective-permute-start(f32[4,128,128]{2,1,0:T(8,128)S(1)} %multiply_add_fusion.5), channel_id=1, source_target_pairs={{4,0},{8,4},{12,8},{16,12},{20,16},{24,20},{28,24},{32,28},{36,32}... | collective-permute-start | bytes 786440 | tf_op jit(solution)/shard_map/while/body/eval_jaxpr/ppermute | solution.py:13
  633.0 17.4 %collective-permute-start.1 = (f32[4,128,128]{2,1,0:T(8,128)S(1)}, f32[4,128,128]{2,1,0:T(8,128)S(1)}, u32[]{:S(2)}, u32[]{:S(2)}) collective-permute-start(f32[4,128,128]{2,1,0:T(8,128)S(1)} %multiply_add_fusion.5), channel_id=1, source_target_pairs={{4,0},{8,4},{12,8},{16,12},{20,16},{24,20},{28,24},{32,28},{36,32}... | collective-permute-start | bytes 786440 | tf_op jit(solution)/shard_map/while/body/eval_jaxpr/ppermute | solution.py:13
  650.6 12.5 %collective-permute-start.1 = (f32[4,128,128]{2,1,0:T(8,128)S(1)}, f32[4,128,128]{2,1,0:T(8,128)S(1)}, u32[]{:S(2)}, u32[]{:S(2)}) collective-permute-start(f32[4,128,128]{2,1,0:T(8,128)S(1)} %multiply_add_fusion.5), channel_id=1, source_target_pairs={{4,0},{8,4},{12,8},{16,12},{20,16},{24,20},{28,24},{32,28},{36,32}... | collective-permute-start | bytes 786440 | tf_op jit(solution)/shard_map/while/body/eval_jaxpr/ppermute | solution.py:13
  663.2 14.0 %collective-permute-start.1 = (f32[4,128,128]{2,1,0:T(8,128)S(1)}, f32[4,128,128]{2,1,0:T(8,128)S(1)}, u32[]{:S(2)}, u32[]{:S(2)}) collective-permute-start(f32[4,128,128]{2,1,0:T(8,128)S(1)} %multiply_add_fusion.5), channel_id=1, source_target_pairs={{4,0},{8,4},{12,8},{16,12},{20,16},{24,20},{28,24},{32,28},{36,32}... | collective-permute-start | bytes 786440 | tf_op jit(solution)/shard_map/while/body/eval_jaxpr/ppermute | solution.py:13
  677.3 11.3 %collective-permute-start.1 = (f32[4,128,128]{2,1,0:T(8,128)S(1)}, f32[4,128,128]{2,1,0:T(8,128)S(1)}, u32[]{:S(2)}, u32[]{:S(2)}) collective-permute-start(f32[4,128,128]{2,1,0:T(8,128)S(1)} %multiply_add_fusion.5), channel_id=1, source_target_pairs={{4,0},{8,4},{12,8},{16,12},{20,16},{24,20},{28,24},{32,28},{36,32}... | collective-permute-start | bytes 786440 | tf_op jit(solution)/shard_map/while/body/eval_jaxpr/ppermute | solution.py:13
  688.7 9.7 collective-permute-start.1
  698.5 12.1 %collective-permute-start.1 = (f32[4,128,128]{2,1,0:T(8,128)S(1)}, f32[4,128,128]{2,1,0:T(8,128)S(1)}, u32[]{:S(2)}, u32[]{:S(2)}) collective-permute-start(f32[4,128,128]{2,1,0:T(8,128)S(1)} %multiply_add_fusion.5), channel_id=1, source_target_pairs={{4,0},{8,4},{12,8},{16,12},{20,16},{24,20},{28,24},{32,28},{36,32}... | collective-permute-start | bytes 786440 | tf_op jit(solution)/shard_map/while/body/eval_jaxpr/ppermute | solution.py:13
  710.6 11.7 %collective-permute-start.1 = (f32[4,128,128]{2,1,0:T(8,128)S(1)}, f32[4,128,128]{2,1,0:T(8,128)S(1)}, u32[]{:S(2)}, u32[]{:S(2)}) collective-permute-start(f32[4,128,128]{2,1,0:T(8,128)S(1)} %multiply_add_fusion.5), channel_id=1, source_target_pairs={{4,0},{8,4},{12,8},{16,12},{20,16},{24,20},{28,24},{32,28},{36,32}... | collective-permute-start | bytes 786440 | tf_op jit(solution)/shard_map/while/body/eval_jaxpr/ppermute | solution.py:13
  722.4 12.2 %collective-permute-start.1 = (f32[4,128,128]{2,1,0:T(8,128)S(1)}, f32[4,128,128]{2,1,0:T(8,128)S(1)}, u32[]{:S(2)}, u32[]{:S(2)}) collective-permute-start(f32[4,128,128]{2,1,0:T(8,128)S(1)} %multiply_add_fusion.5), channel_id=1, source_target_pairs={{4,0},{8,4},{12,8},{16,12},{20,16},{24,20},{28,24},{32,28},{36,32}... | collective-permute-start | bytes 786440 | tf_op jit(solution)/shard_map/while/body/eval_jaxpr/ppermute | solution.py:13
  734.8 10.9 %collective-permute-start.1 = (f32[4,128,128]{2,1,0:T(8,128)S(1)}, f32[4,128,128]{2,1,0:T(8,128)S(1)}, u32[]{:S(2)}, u32[]{:S(2)}) collective-permute-start(f32[4,128,128]{2,1,0:T(8,128)S(1)} %multiply_add_fusion.5), channel_id=1, source_target_pairs={{4,0},{8,4},{12,8},{16,12},{20,16},{24,20},{28,24},{32,28},{36,32}... | collective-permute-start | bytes 786440 | tf_op jit(solution)/shard_map/while/body/eval_jaxpr/ppermute | solution.py:13
  745.8 11.5 %collective-permute-start.1 = (f32[4,128,128]{2,1,0:T(8,128)S(1)}, f32[4,128,128]{2,1,0:T(8,128)S(1)}, u32[]{:S(2)}, u32[]{:S(2)}) collective-permute-start(f32[4,128,128]{2,1,0:T(8,128)S(1)} %multiply_add_fusion.5), channel_id=1, source_target_pairs={{4,0},{8,4},{12,8},{16,12},{20,16},{24,20},{28,24},{32,28},{36,32}... | collective-permute-start | bytes 786440 | tf_op jit(solution)/shard_map/while/body/eval_jaxpr/ppermute | solution.py:13
  757.4 12.5 %collective-permute-start.1 = (f32[4,128,128]{2,1,0:T(8,128)S(1)}, f32[4,128,128]{2,1,0:T(8,128)S(1)}, u32[]{:S(2)}, u32[]{:S(2)}) collective-permute-start(f32[4,128,128]{2,1,0:T(8,128)S(1)} %multiply_add_fusion.5), channel_id=1, source_target_pairs={{4,0},{8,4},{12,8},{16,12},{20,16},{24,20},{28,24},{32,28},{36,32}... | collective-permute-start | bytes 786440 | tf_op jit(solution)/shard_map/while/body/eval_jaxpr/ppermute | solution.py:13
  858.8 109.4 %copy-start.19 = (f32[2,4,512]{2,1,0:T(4,128)}, f32[2,4,512]{2,1,0:T(4,128)S(1)}, u32[]{:S(2)}) copy-start(f32[2,4,512]{2,1,0:T(4,128)S(1)} %get-tuple-element.489) | copy-start | bytes 49156
  (33 other events, 377.7 us)
Sparse Core Ops, SparseCore 0:
  961.2 13.3 reduce-scatter.3
